TPU v7x, 128 devices: a whole 4x4x4 slice. The times are simulated.
128 devices in a mesh: seq: 16 (over y_lo, x, core), head: 8 (over y_hi, z).
Axes of the slice: x: 4, y: 4 (y_hi: 2, y_lo: 2; y = y_hi * 2 + y_lo), z: 4, core: 2. Of those that a mesh axis runs over, the one named last changes fastest.
Arguments:
- video_in: bfloat16 [10240, 3072], P('seq'), may hold values from -6 to 6
- text_in: bfloat16 [256, 3072], P('seq'), may hold values from -6 to 6
- mod_video: float32 [3, 3072], replicated, may hold values from -4 to 4
- mod_text: float32 [3, 3072], replicated, may hold values from -4 to 4
- qkv_video: bfloat16 [3072, 3, 3072], P('seq', None, 'head'), may hold values from -0.109375 to 0.109375
- qkv_text: bfloat16 [3072, 3, 3072], P('seq', None, 'head'), may hold values from -0.109375 to 0.109375
- proj_video: bfloat16 [3072, 3072], P('head', 'seq'), may hold values from -0.15625 to 0.15625
- proj_text: bfloat16 [3072, 3072], P('head', 'seq'), may hold values from -0.15625 to 0.15625
- gain_video: float32 [2, 128], replicated, may hold values from 1.5 to 12
- gain_text: float32 [2, 128], replicated, may hold values from 1.5 to 12
- windows: int32 [24, 3], replicated, may hold values from 0 to 4, as said below
- text_len: int32 [1], replicated, may hold values from 64 to 256
Outputs:
- video_out: bfloat16 [10240, 3072], P('seq', 'head')
- text_out: bfloat16 [256, 3072], P('seq', 'head')
Inputs may be any that keep to these rules, and one draw needn't show every extreme that they name: `windows`: row h holds head h's half-widths: time tiles 0 to 1, height tiles 0 to 1, width tiles 0 to 4; some head has all three at their largest.
All inputs are finite; a program needn't handle non-finite values.
Results may differ from a plain program's by a relative error of at most 0.014.
The roundings to bfloat16 on the way count: a program that leaves them out, or rounds other values in their place, can miss the bound.
Values may be sent and summed in bfloat16 or wider, within the bound.
A program may use at most 128 MiB of HBM per device.

v0:
```python
import jax
import jax.numpy as jnp
from jax import lax
from jax.sharding import PartitionSpec as P

FRAMES = 4
TT = 2
TH = 4
TW = 16
W = 80
HT_DEV = 1


NEG_BIG = -1e30


def passed_along(shard, axis, by):
    length = lax.axis_size(axis)
    pairs = [(i, i + by) for i in range(length) if 0 <= i + by < length]
    return lax.ppermute(shard, axis, pairs)


def joined(part, axis, combine):
    gathered = jax.tree.map(lambda a: lax.all_gather(a, axis), part)

    def take(source):
        return jax.tree.map(lambda a: lax.dynamic_index_in_dim(a, source, 0, False), gathered)

    return lax.fori_loop(
        1, lax.axis_size(axis), lambda source, state: combine(state, take(source)), take(0)
    )


def modulate(tokens, modulation):
    values = tokens.astype(jnp.float32)
    center = jnp.mean(values, axis=1, keepdims=True)
    spread = jnp.mean(jnp.square(values - center), axis=1, keepdims=True)
    normed = (values - center) * lax.rsqrt(spread + 1e-06)
    return (normed * (1.0 + modulation[1]) + modulation[0]).astype(jnp.bfloat16)


def head_norm(values, gains_row, head_size):
    row_count = values.shape[0]
    by_head = values.reshape(row_count, -1, head_size)
    scaled = (
        by_head
        * lax.rsqrt(jnp.mean(jnp.square(by_head), axis=2, keepdims=True) + 1e-06)
        * gains_row
    )
    return scaled.reshape(row_count, -1).astype(jnp.bfloat16)


def finish_qkv(projected, gains, head_size):
    return (
        head_norm(projected[:, 0], gains[0], head_size),
        head_norm(projected[:, 1], gains[1], head_size),
        projected[:, 2].astype(jnp.bfloat16),
    )


def tile_coords(block_index, row_count, hblocks):
    positions = jnp.arange(row_count, dtype=jnp.int32)
    t_tile = jnp.zeros((row_count,), jnp.int32) + block_index // hblocks
    h_tile = block_index % hblocks * HT_DEV + positions % (HT_DEV * TH * W) // (W * TH)
    w_tile = positions % W // TW
    return (t_tile, h_tile, w_tile)


def window_mask(query_pos, key_pos, spans):
    inside_all = None
    for number in range(3):
        distance = jnp.abs(query_pos[number][:, None] - key_pos[number][None, :])
        inside = distance[None, :, :] <= spans[:, number][:, None, None]
        inside_all = inside if inside_all is None else inside_all & inside
    return inside_all


def attend_block(running, queries, key_vecs, value_vecs, allowed):
    row_max, row_sum, summed = running
    scores = jnp.einsum(
        "qhd,khd->hqk", queries, key_vecs, preferred_element_type=jnp.float32
    ) * queries.shape[2] ** (-0.5)
    scores = jnp.where(allowed, scores, NEG_BIG)
    new_max = jnp.maximum(row_max, jnp.max(scores, axis=2))
    factor = jnp.exp(row_max - new_max)
    powers = jnp.where(allowed, jnp.exp(scores - new_max[:, :, None]), 0.0)
    row_sum = row_sum * factor + jnp.sum(powers, axis=2)
    summed = summed * factor[:, :, None] + jnp.einsum(
        "hqk,khd->hqd", powers.astype(jnp.bfloat16), value_vecs, preferred_element_type=jnp.float32
    )
    return (new_max, row_sum, summed)


def combine(earlier, later):
    joint_max = jnp.maximum(earlier[0], later[0])
    weight_one = jnp.exp(earlier[0] - joint_max)
    weight_two = jnp.exp(later[0] - joint_max)
    return (
        joint_max,
        earlier[1] * weight_one + later[1] * weight_two,
        earlier[2] * weight_one[:, :, None] + later[2] * weight_two[:, :, None],
    )


def empty_state(head_count, row_count, head_size):
    return (
        jnp.full((head_count, row_count), NEG_BIG, jnp.float32),
        jnp.zeros((head_count, row_count), jnp.float32),
        jnp.zeros((head_count, row_count, head_size), jnp.float32),
    )


def body(
    video_in,
    text_in,
    mod_video,
    mod_text,
    qkv_video,
    qkv_text,
    proj_video,
    proj_text,
    gain_video,
    gain_text,
    windows,
    text_len,
):
    head_size = gain_video.shape[1]
    seq_count = lax.axis_size("seq")
    seq_index = lax.axis_index("seq")
    head_index = lax.axis_index("head")
    hblocks = seq_count // (FRAMES // TT)
    local_width = qkv_video.shape[2]
    local_heads = local_width // head_size
    vid_rows = video_in.shape[0]
    txt_rows = text_in.shape[0]
    spans = lax.dynamic_slice_in_dim(windows, head_index * local_heads, local_heads, 0)
    normed_video = modulate(video_in, mod_video)
    normed_text = modulate(text_in, mod_text)
    columns = normed_video
    proj_v = jnp.einsum(
        "rc,cgn->rgn",
        columns,
        lax.all_gather(qkv_video, "seq", axis=0, tiled=True),
        preferred_element_type=jnp.float32,
    )
    columns = normed_text
    proj_t = jnp.einsum(
        "rc,cgn->rgn",
        columns,
        lax.all_gather(qkv_text, "seq", axis=0, tiled=True),
        preferred_element_type=jnp.float32,
    )
    query_v, key_v, value_v = finish_qkv(proj_v, gain_video, head_size)
    query_t, key_t, value_t = finish_qkv(proj_t, gain_text, head_size)
    all_query_t, all_key_t, all_value_t = (
        lax.all_gather(query_t, "seq", axis=0, tiled=True),
        lax.all_gather(key_t, "seq", axis=0, tiled=True),
        lax.all_gather(value_t, "seq", axis=0, tiled=True),
    )
    txt_total = all_key_t.shape[0]
    text_ok = jnp.arange(txt_total, dtype=jnp.int32) < text_len[0]
    text_keys = all_key_t.reshape(txt_total, local_heads, head_size)
    text_values = all_value_t.reshape(txt_total, local_heads, head_size)
    key_value = jnp.stack([key_v, value_v])
    relative = [t_off + h_off for t_off in (0, -hblocks, hblocks) for h_off in (0, -1, 1)]
    key_blocks = jnp.stack(
        [key_value] + [passed_along(key_value, "seq", -offset) for offset in relative[1:]]
    )
    query_pos = tile_coords(seq_index, vid_rows, hblocks)
    video_queries = query_v.reshape(vid_rows, local_heads, head_size)

    def video_block(running, inputs):
        block_pair, relative_source = inputs
        source = seq_index + relative_source
        present = (source >= 0) & (source < seq_count)
        key_pos = tile_coords(jnp.clip(source, 0, seq_count - 1), vid_rows, hblocks)
        allowed = window_mask(query_pos, key_pos, spans) & present
        key_vecs = block_pair[0].reshape(vid_rows, local_heads, head_size)
        value_vecs = block_pair[1].reshape(vid_rows, local_heads, head_size)
        return (attend_block(running, video_queries, key_vecs, value_vecs, allowed), None)

    running, unused = lax.scan(
        video_block,
        empty_state(local_heads, vid_rows, head_size),
        (key_blocks, jnp.array(relative, jnp.int32)),
    )
    text_allowed = jnp.broadcast_to(text_ok[None, None, :], (local_heads, vid_rows, txt_total))
    row_max, row_sum, summed = attend_block(
        running, video_queries, text_keys, text_values, text_allowed
    )
    attended_v = (
        jnp.transpose(summed / row_sum[:, :, None], (1, 0, 2))
        .reshape(vid_rows, local_width)
        .astype(jnp.bfloat16)
    )
    text_queries = all_query_t.reshape(txt_total, local_heads, head_size)
    every_key = jnp.ones((local_heads, txt_total, vid_rows), bool)
    local_part = attend_block(
        empty_state(local_heads, txt_total, head_size),
        text_queries,
        key_v.reshape(vid_rows, local_heads, head_size),
        value_v.reshape(vid_rows, local_heads, head_size),
        every_key,
    )
    merged = joined(local_part, "seq", combine)
    text_self = jnp.broadcast_to(text_ok[None, None, :], (local_heads, txt_total, txt_total))
    text_max, text_sum, text_summed = attend_block(
        merged, text_queries, text_keys, text_values, text_self
    )
    own_rows = lax.dynamic_slice_in_dim(
        text_summed / text_sum[:, :, None], seq_index * txt_rows, txt_rows, 1
    )
    attended_t = (
        jnp.transpose(own_rows, (1, 0, 2)).reshape(txt_rows, local_width).astype(jnp.bfloat16)
    )
    branch_video = jnp.dot(
        attended_v,
        lax.all_gather(proj_video, "seq", axis=1, tiled=True),
        preferred_element_type=jnp.float32,
    )
    branch_text = jnp.dot(
        attended_t,
        lax.all_gather(proj_text, "seq", axis=1, tiled=True),
        preferred_element_type=jnp.float32,
    )
    sum_video, sum_text = (
        lax.psum_scatter(
            branch_video.astype(jnp.bfloat16), "head", scatter_dimension=1, tiled=True
        ).astype(jnp.float32),
        lax.psum_scatter(
            branch_text.astype(jnp.bfloat16), "head", scatter_dimension=1, tiled=True
        ).astype(jnp.float32),
    )
    out_width = sum_video.shape[1]
    col_start = head_index * out_width
    resid_video = lax.dynamic_slice_in_dim(video_in, col_start, out_width, 1).astype(jnp.float32)
    resid_text = lax.dynamic_slice_in_dim(text_in, col_start, out_width, 1).astype(jnp.float32)
    gate_video = lax.dynamic_slice_in_dim(mod_video[2], col_start, out_width, 0)
    gate_text = lax.dynamic_slice_in_dim(mod_text[2], col_start, out_width, 0)
    video_out = (resid_video + gate_video * sum_video).astype(jnp.bfloat16)
    text_out = (resid_text + gate_text * sum_text).astype(jnp.bfloat16)
    return (video_out, text_out)


def solution(mesh):
    return jax.shard_map(
        body,
        mesh=mesh,
        in_specs=(
            P("seq", None),
            P("seq", None),
            P(),
            P(),
            P("seq", None, "head"),
            P("seq", None, "head"),
            P("head", "seq"),
            P("head", "seq"),
            P(),
            P(),
            P(),
            P(),
        ),
        out_specs=(P("seq", "head"), P("seq", "head")),
        check_vma=False,
    )
```

profile of v0, /device:TPU:1, one launch (start us, length us, event | category | flops | bytes accessed | tf_op | source)
XLA Modules:
  0.0 685.3 jit_solution(5569016894922365684)
XLA Ops:
  15.2 2.7 convert_reduce_fusion
  20.0 39.3 %all-gather.12.cloned.1.call-done = bf16[3072,3,384]{2,0,1:T(8,128)(2,1)} async-done(((bf16[192,3,384]{2,0,1:T(8,128)(2,1)}), bf16[3072,3,384]{2,0,1:T(8,128)(2,1)}) %all-gather.12.cloned.1.call-update) | async-done | bytes 7077904 | tf_op jit(solution)/shard_map/all_gather | solution.py:150
  59.3 4.1 fusion.82
  63.4 44.4 %all-gather.10.cloned.1.call-done = bf16[3072,3,384]{2,0,1:T(8,128)(2,1)} async-done(((bf16[192,3,384]{2,0,1:T(8,128)(2,1)}), bf16[3072,3,384]{2,0,1:T(8,128)(2,1)}) %all-gather.10.cloned.1.call-update) | async-done | bytes 7077904 | tf_op jit(solution)/shard_map/all_gather | solution.py:143
  107.8 10.7 %fusion.40 = f32[640,3,384]{0,2,1:T(8,128)S(1)} fusion(bf16[3072,3,384]{2,0,1:T(8,128)(2,1)} %all-gather.10.cloned.1.call-done, bf16[640,3072]{1,0:T(8,128)(2,1)} %param.17, f32[3072]{0:T(1024)S(1)} %bitcast.207, f32[3072]{0:T(1024)S(1)} %bitcast.208, f32[640]{0:T(1024)S(1)} %add_rsqrt_fusion.4, f32[640]{0:T(1024)S(1)} %broadcast_multiply_fusion), kind=kOutput, calls=%fused_computation.68 | convolution fusion | flops 4541644800 | bytes 13988864 | tf_op jit(solution)/shard_map/rc,cgn->rgn/dot_general | solution.py:140
  121.1 3.2 collective-permute-start
  126.4 3.9 collective-permute-start.2
  130.3 2.7 collective-permute-start.3
  133.0 2.8 collective-permute-start.4
  136.7 37.6 %all_gather.37 = bf16[256,384]{1,0:T(8,128)(2,1)S(1)} all-gather(bf16[16,384]{1,0:T(8,128)(2,1)S(1)} %get-tuple-element.534), channel_id=1, replica_groups=mesh['seq'=16,'head'=8] {'seq'}, dimensions={0}, use_global_device_ids=true | all-gather | bytes 208896 | tf_op jit(solution)/shard_map/all_gather | solution.py:157
  177.3 16.9 %all-gather = bf16[256,1,384]{2,0,1:T(8,128)(2,1)S(1)} all-gather(bf16[16,1,384]{2,0,1:T(8,128)(2,1)S(1)} %slice.149), channel_id=2, replica_groups=mesh['seq'=16,'head'=8] {'seq'}, dimensions={0}, use_global_device_ids=true | all-gather | bytes 208896 | tf_op jit(solution)/shard_map/all_gather | solution.py:158
  206.1 24.9 %collective-permute-done.5 = bf16[2,640,384]{1,2,0:T(8,128)(2,1)S(1)} collective-permute-done((bf16[2,640,384]{1,2,0:T(8,128)(2,1)}, bf16[2,640,384]{1,2,0:T(8,128)(2,1)S(1)}, u32[]{:S(2)}, u32[]{:S(2)}) %collective-permute-start.5) | collective-permute-done | bytes 983072 | tf_op jit(solution)/shard_map/ppermute | solution.py:20
  231.2 21.2 %collective-permute-done.6 = bf16[2,640,384]{1,2,0:T(8,128)(2,1)S(1)} collective-permute-done((bf16[2,640,384]{1,2,0:T(8,128)(2,1)}, bf16[2,640,384]{1,2,0:T(8,128)(2,1)S(1)}, u32[]{:S(2)}, u32[]{:S(2)}) %collective-permute-start.6) | collective-permute-done | bytes 983072 | tf_op jit(solution)/shard_map/ppermute | solution.py:20
  252.7 3.4 copy-done.8
  256.1 156.0 %while.39 = (s32[]{:T(128)}, f32[3,640]{1,0:T(4,128)S(1)}, f32[3,640]{1,0:T(4,128)S(1)}, f32[3,640,128]{2,1,0:T(8,128)}, s32[]{:T(128)}, /*index=5*/s32[3,3]{0,1...) while((s32[]{:T(128)}, f32[3,640]{1,0:T(4,128)S(1)}, ...), condition=%wide.region_7.0_spmd.clone.clone, body=%wide.region_4.7_spmd.sunk.clone.clone.sunk | while | flops 653672960 | bytes 58056460 | solution.py:182
  259.7 6.1 fusion.146
  265.8 4.0 fusion.147
  277.1 6.1 fusion.146
  283.1 4.0 fusion.147
  287.3 2.5 fusion.149
  294.4 6.1 fusion.146
  300.5 4.0 fusion.147
  304.6 2.5 fusion.149
  311.7 6.1 fusion.146
  317.8 4.0 fusion.147
  329.1 6.1 fusion.146
  335.1 4.0 fusion.147
  339.3 2.5 fusion.149
  346.4 6.1 fusion.146
  352.5 4.0 fusion.147
  356.6 2.5 fusion.149
  363.7 6.1 fusion.146
  369.8 4.0 fusion.147
  381.1 6.1 fusion.146
  387.2 4.0 fusion.147
  391.3 2.5 fusion.149
  398.4 6.1 fusion.146
  404.5 4.0 fusion.147
  417.5 5.9 convolution_convert_fusion
  423.4 6.2 copy.79
  432.4 28.9 %all_gather.40 = bf16[256,384]{1,0:T(8,128)(2,1)S(1)} all-gather(bf16[16,384]{1,0:T(8,128)(2,1)S(1)} %get-tuple-element.533), channel_id=1, replica_groups=mesh['seq'=16,'head'=8] {'seq'}, dimensions={0}, use_global_device_ids=true | all-gather | bytes 208896 | tf_op jit(solution)/shard_map/all_gather | solution.py:156
  465.8 16.6 %all_gather.42 = f32[16,3,256]{2,1,0:T(4,128)S(1)} all-gather(f32[1,3,256]{2,1,0:T(4,128)S(1)} %get-tuple-element.544), channel_id=1, replica_groups=mesh['seq'=16,'head'=8] {'seq'}, dimensions={0}, use_global_device_ids=true | all-gather | bytes 52224 | tf_op jit(solution)/shard_map/all_gather | solution.py:24
  482.4 17.6 %all-gather.3 = f32[16,3,256]{2,1,0:T(4,128)S(1)} all-gather(f32[1,3,256]{2,1,0:T(4,128)S(1)} %get-tuple-element.545), channel_id=3, replica_groups=mesh['seq'=16,'head'=8] {'seq'}, dimensions={0}, use_global_device_ids=true | all-gather | bytes 52224 | tf_op jit(solution)/shard_map/all_gather | solution.py:24
  500.1 21.6 %reduce-scatter.7.cloned.1.call-done = bf16[384,640]{1,0:T(8,128)(2,1)} async-done(((bf16[3072,640]{1,0:T(8,128)(2,1)}), bf16[384,640]{1,0:T(8,128)(2,1)}) %reduce-scatter.7.cloned.1.call-update) | async-done | bytes 491536
  523.0 43.5 %all-gather.18.cloned.1.call-done = f32[48,256,128]{2,1,0:T(8,128)} async-done(((f32[3,256,128]{2,1,0:T(8,128)}), f32[48,256,128]{2,1,0:T(8,128)}) %all-gather.18.cloned.1.call-update) | async-done | bytes 6291472 | tf_op jit(solution)/shard_map/all_gather | solution.py:24
  567.5 21.2 %while.38 = (s32[]{:T(128)}, f32[3,256]{1,0:T(4,128)S(1)}, f32[3,256]{1,0:T(4,128)S(1)}, f32[3,256,128]{2,1,0:T(8,128)S(1)}, f32[16,3,256]{2,1,0:T(4,128)S(1)}, ...) while((s32[]{:T(128)}, f32[3,256]{1,0:T(4,128)S(1)}, ...), condition=%wide.region_18.19_spmd, body=%wide.region_17.18_spmd.sunk | while | flops 299525 | bytes 1210519 | solution.py:29
  589.5 13.8 %all-gather.16.cloned.1.call-done = bf16[384,3072]{0,1:T(8,128)(2,1)} async-done(((bf16[384,192]{0,1:T(8,128)(2,1)}), bf16[384,3072]{0,1:T(8,128)(2,1)}) %all-gather.16.cloned.1.call-update) | async-done | bytes 2359312 | tf_op jit(solution)/shard_map/all_gather | solution.py:223
  608.9 68.0 %reduce-scatter.9.cloned.1.call-done = bf16[384,16]{1,0:T(8,128)(2,1)} async-done(((bf16[3072,16]{1,0:T(8,128)(2,1)}), bf16[384,16]{1,0:T(8,128)(2,1)}) %reduce-scatter.9.cloned.1.call-update) | async-done | bytes 12304
  (344 shorter events, 120.2 us)
Async XLA Ops:
  7.2 12.7 %copy-start = (s32[24,3]{0,1:T(4,128)S(1)}, s32[24,3]{0,1:T(4,128)}, u32[]{:S(2)}) copy-start(s32[24,3]{0,1:T(4,128)} %param.27) | copy-start | bytes 868
  7.2 52.1 %all-gather.12.cloned.1.call-start = ((), (), s32[]{:S(2)}) async-start(), calls=%async_computation.3 | async-start | bytes 7520256 | tf_op jit(solution)/shard_map/all_gather | solution.py:150
  7.9 99.9 %all-gather.10.cloned.1.call-start = ((), (), s32[]{:S(2)}) async-start(), calls=%async_computation.2 | async-start | bytes 7520256 | tf_op jit(solution)/shard_map/all_gather | solution.py:143
  8.7 408.8 %all-gather.14.cloned.1.call-start = ((), (), s32[]{:S(2)}) async-start(), calls=%async_computation.4 | async-start | bytes 2506752 | tf_op jit(solution)/shard_map/all_gather | solution.py:218
  9.4 512.3 %reduce-scatter.7.cloned.1.call-start = ((), (), s32[]{:S(2)}) async-start(), calls=%async_computation.7 | async-start | bytes 4423680
  9.5 8.5 %copy-start.3 = (bf16[640,3072]{1,0:T(8,128)(2,1)S(1)}, bf16[640,3072]{1,0:T(8,128)(2,1)}, u32[]{:S(2)}) copy-start(bf16[640,3072]{1,0:T(8,128)(2,1)} %param.17) | copy-start | bytes 11796484
  15.2 3.9 copy-start.18
  15.2 44.1 %copy-start.14 = (bf16[16,3072]{1,0:T(8,128)(2,1)S(1)}, bf16[16,3072]{1,0:T(8,128)(2,1)}, u32[]{:S(2)}) copy-start(bf16[16,3072]{1,0:T(8,128)(2,1)} %param.18) | copy-start | bytes 294916
  19.1 40.1 %copy-start.16 = (f32[128]{0:T(128)}, f32[128]{0:T(128)S(1)}, u32[]{:S(2)}) copy-start(f32[128]{0:T(128)S(1)} %get-tuple-element.548) | copy-start | bytes 1540
  121.1 74.1 %collective-permute-start = (bf16[2,640,384]{1,2,0:T(8,128)(2,1)}, bf16[2,640,384]{1,2,0:T(8,128)(2,1)}, u32[]{:S(2)}, u32[]{:S(2)}) collective-permute-start(bf16[2,640,384]{1,2,0:T(8,128)(2,1)} %pad_maximum_fusion), channel_id=1, source_target_pairs={{0,8},{8,16},{16,24},{24,32},{32,40},{40,48},{48,56},{56,64},{64,7... | collective-permute-start | bytes 2949128 | tf_op jit(solution)/shard_map/ppermute | solution.py:20
  124.2 73.6 %collective-permute-start.1 = (bf16[2,640,384]{1,2,0:T(8,128)(2,1)}, bf16[2,640,384]{1,2,0:T(8,128)(2,1)}, u32[]{:S(2)}, u32[]{:S(2)}) collective-permute-start(bf16[2,640,384]{1,2,0:T(8,128)(2,1)} %pad_maximum_fusion), channel_id=1, source_target_pairs={{8,0},{16,8},{24,16},{32,24},{40,32},{48,40},{56,48},{64,56},{72,6... | collective-permute-start | bytes 2949128 | tf_op jit(solution)/shard_map/ppermute | solution.py:20
  126.4 74.1 %collective-permute-start.2 = (bf16[2,640,384]{1,2,0:T(8,128)(2,1)}, bf16[2,640,384]{1,2,0:T(8,128)(2,1)}, u32[]{:S(2)}, u32[]{:S(2)}) collective-permute-start(bf16[2,640,384]{1,2,0:T(8,128)(2,1)} %pad_maximum_fusion), channel_id=1, source_target_pairs={{0,64},{8,72},{16,80},{24,88},{32,96},{40,104},{48,112},{56,120},{... | collective-permute-start | bytes 2949128 | tf_op jit(solution)/shard_map/ppermute | solution.py:20
  130.3 73.1 %collective-permute-start.3 = (bf16[2,640,384]{1,2,0:T(8,128)(2,1)}, bf16[2,640,384]{1,2,0:T(8,128)(2,1)}, u32[]{:S(2)}, u32[]{:S(2)}) collective-permute-start(bf16[2,640,384]{1,2,0:T(8,128)(2,1)} %pad_maximum_fusion), channel_id=1, source_target_pairs={{0,72},{8,80},{16,88},{24,96},{32,104},{40,112},{48,120},{1,73},{9... | collective-permute-start | bytes 2949128 | tf_op jit(solution)/shard_map/ppermute | solution.py:20
  133.0 71.7 %collective-permute-start.4 = (bf16[2,640,384]{1,2,0:T(8,128)(2,1)}, bf16[2,640,384]{1,2,0:T(8,128)(2,1)}, u32[]{:S(2)}, u32[]{:S(2)}) collective-permute-start(bf16[2,640,384]{1,2,0:T(8,128)(2,1)} %pad_maximum_fusion), channel_id=1, source_target_pairs={{0,56},{8,64},{16,72},{24,80},{32,88},{40,96},{48,104},{56,112},{6... | collective-permute-start | bytes 2949128 | tf_op jit(solution)/shard_map/ppermute | solution.py:20
  174.4 23.4 %copy-start.10 = (bf16[256,384]{0,1:T(8,128)(2,1)}, bf16[256,384]{0,1:T(8,128)(2,1)S(1)}, u32[]{:S(2)}) copy-start(bf16[256,384]{0,1:T(8,128)(2,1)S(1)} %copy.54) | copy-start | bytes 589828
  195.2 35.8 %collective-permute-start.5 = (bf16[2,640,384]{1,2,0:T(8,128)(2,1)}, bf16[2,640,384]{1,2,0:T(8,128)(2,1)S(1)}, u32[]{:S(2)}, u32[]{:S(2)}) collective-permute-start(bf16[2,640,384]{1,2,0:T(8,128)(2,1)} %pad_maximum_fusion), channel_id=1, source_target_pairs={{64,0},{72,8},{80,16},{88,24},{96,32},{104,40},{112,48},{120,56},{... | collective-permute-start | bytes 2949128 | tf_op jit(solution)/shard_map/ppermute | solution.py:20
  197.8 54.5 %collective-permute-start.6 = (bf16[2,640,384]{1,2,0:T(8,128)(2,1)}, bf16[2,640,384]{1,2,0:T(8,128)(2,1)S(1)}, u32[]{:S(2)}, u32[]{:S(2)}) collective-permute-start(bf16[2,640,384]{1,2,0:T(8,128)(2,1)} %pad_maximum_fusion), channel_id=1, source_target_pairs={{56,0},{64,8},{72,16},{80,24},{88,32},{96,40},{104,48},{112,56},{1... | collective-permute-start | bytes 2949128 | tf_op jit(solution)/shard_map/ppermute | solution.py:20
  200.5 52.0 %collective-permute-start.7 = (bf16[2,640,384]{1,2,0:T(8,128)(2,1)}, bf16[2,640,384]{1,2,0:T(8,128)(2,1)S(1)}, u32[]{:S(2)}, u32[]{:S(2)}) collective-permute-start(bf16[2,640,384]{1,2,0:T(8,128)(2,1)} %pad_maximum_fusion), channel_id=1, source_target_pairs={{72,0},{80,8},{88,16},{96,24},{104,32},{112,40},{120,48},{73,1},{8... | collective-permute-start | bytes 2949128 | tf_op jit(solution)/shard_map/ppermute | solution.py:20
  204.7 51.4 %copy-start.19 = (s32[9]{0:T(128)S(1)}, s32[9]{0:T(128)}, u32[]{:S(2)}) copy-start(s32[9]{0:T(128)} %constant.311.clone..sunk.3) | copy-start | bytes 112
  265.8 4.1 copy-start.12
  265.8 4.2 copy-start.2
  283.1 4.1 copy-start.12
  283.1 4.2 copy-start.2
  287.3 3.5 copy-start.20
  300.5 4.1 copy-start.12
  300.5 4.2 copy-start.2
  304.6 3.5 copy-start.20
  317.8 4.1 copy-start.12
  317.8 4.2 copy-start.2
  335.1 4.1 copy-start.12
  335.1 4.2 copy-start.2
  352.5 4.1 copy-start.12
  352.5 4.2 copy-start.2
  356.6 3.5 copy-start.20
  369.8 4.1 copy-start.12
  369.8 4.2 copy-start.2
  387.1 4.1 copy-start.12
  387.1 4.2 copy-start.2
  404.5 4.1 copy-start.12
  404.5 4.2 copy-start.2
  412.1 3.8 copy-start.6
  412.1 3.8 copy-start.15
  429.6 31.8 %copy-start.17 = (f32[128]{0:T(128)S(1)}, f32[128]{0:T(128)}, u32[]{:S(2)}) copy-start(f32[128]{0:T(128)} %copy-done.16) | copy-start | bytes 1540
  429.6 136.9 %all-gather.18.cloned.1.call-start = ((), (), s32[]{:S(2)}) async-start(), calls=%async_computation.6 | async-start | bytes 6684672 | tf_op jit(solution)/shard_map/all_gather | solution.py:24
  461.4 4.0 copy-start.11
  464.1 139.1 %all-gather.16.cloned.1.call-start = ((), (), s32[]{:S(2)}) async-start(), calls=%async_computation.5 | async-start | bytes 2506752 | tf_op jit(solution)/shard_map/all_gather | solution.py:223
  464.7 212.1 %reduce-scatter.9.cloned.1.call-start = ((), (), s32[]{:S(2)}) async-start(), calls=%async_computation.8 | async-start | bytes 884736
  588.7 89.7 %copy-start.1 = (s32[24,3]{0,1:T(4,128)S(1)}, s32[24,3]{0,1:T(4,128)}, u32[]{:S(2)}) copy-start(s32[24,3]{0,1:T(4,128)} %param.27) | copy-start | bytes 868
  (20 other events, 38.7 us)
Sparse Core Ops, SparseCore 0:
  9.7 49.5 all-gather.11
  60.9 46.8 all-gather.9
  109.5 56.6 all-gather.13
  429.8 91.9 reduce-scatter.6
  523.9 42.5 all-gather.17
  568.2 35.0 all-gather.15
  607.2 69.5 reduce-scatter.8
where the time goes:
time: 688 us; the launch traced here: 685 us
  waiting for transfers between devices  279 us (41%)
  blocking collectives  118 us (17%)
  matrix products  106 us (15%)
  other arithmetic  84 us (12%)
  local copies, waits for them, and re-layouts  57.1 us (8%)
  starting transfers between devices  19.1 us (3%)
  between operations  15.4 us (2%)
    unnamed x9, waiting for transfers between devices  92.2 us
    dot_general x12, matrix products, attend_block(): jnp.einsum('qhd,khd->hqk', queries, key_vecs, preferred_element_type=jnp....  57.5 us
    ppermute x8, waiting for transfers between devices, passed_along(): return lax.ppermute(shard, axis, pairs)  46.1 us
    all_gather x1, waiting for transfers between devices, body(): lax.all_gather(qkv_video, 'seq', axis=0, tiled=True)  44.4 us
    all_gather x1, waiting for transfers between devices, joined(): gathered = jax.tree.map(lambda a: lax.all_gather(a, axis), part)  43.5 us
    all_gather x1, waiting for transfers between devices, body(): lax.all_gather(qkv_text, 'seq', axis=0, tiled=True)  39.3 us
    reduce_sum x12, other arithmetic, attend_block(): row_sum = row_sum * factor + jnp.sum(powers, axis=2)  39 us
    all_gather x1, blocking collectives, body(): lax.all_gather(key_t, 'seq', axis=0, tiled=True)  37.6 us
  transfers between devices with their start and end apart: 15, of which 8 were waited for; matrix products, arithmetic and copies ran while one was open for 31% of the time, Pallas kernels for 0%

commit v1 on v0

v1 whole, which is shorter than its diff:
```python
import math

import jax
import jax.numpy as jnp
from jax import lax
from jax.experimental import pallas as pl
from jax.experimental.pallas import tpu as pltpu
from jax.sharding import PartitionSpec as P

MESH = pl.DeviceIdType.MESH
BF = jnp.bfloat16
F32 = jnp.float32
ROWS = 640
WIDE = 1152
PART = 384
SHARD = 192
HD = 128
TILES = 5
NEG_BIG = -1e30
SCALE2 = math.log2(math.e) / math.sqrt(HD)

GATHER = ("PO", "Y", "L", "R", "LY", "RY", "Da", "Db", "DYa", "DYb",
          "PY", "PL", "PR", "PLY", "PRY", "PDa", "PDb", "PDYa", "PDYb")
GID = {k: i for i, k in enumerate(GATHER)}
RING = ("Up", "Dn", "H", "HUp", "HDn", "D2a", "D2b", "HD2a", "HD2b")
RID = {k: i for i, k in enumerate(RING)}


def remote(src, dst, send, recv, seq=None, head=None):
    to = {}
    if seq is not None:
        to["seq"] = seq
    if head is not None:
        to["head"] = head
    return pltpu.make_async_remote_copy(
        src_ref=src, dst_ref=dst, send_sem=send, recv_sem=recv,
        device_id=to, device_id_type=MESH)


def head_normed(vals, gain):
    return vals * lax.rsqrt(jnp.mean(jnp.square(vals), axis=1, keepdims=True) + 1e-6) * gain


def with_ones(value):
    return jnp.concatenate([value, jnp.ones_like(value)], axis=1)


def kernel(vid, txt, modv, modt, w, wt, pv, pt, gainv, gaint, windows, text_len,
           video_out, text_out,
           normed, wbuf, acc, nt, tnt, part, ppart, tsum_in, tall,
           q, kv, kvbuf, top, att, attbuf, wp, acc2,
           ts, ts_in, atg, tpart, tpart_in,
           own_sem, send, recv, tsend, trecv, rsend, rrecv, gsend, grecv,
           ksend, krecv, zsend, zrecv, wsend, wrecv, psend, precv,
           msend, mrecv, asend, arecv, osend, orecv):
    s = lax.axis_index("seq")
    h = lax.axis_index("head")
    y, x, c = s // 8, (s % 8) // 2, s % 2
    z, yh = h % 4, h // 4
    chip = y * 4 + x

    def seq_of(y, x, c):
        return y * 8 + x * 2 + c

    partner = seq_of(y, x, 1 - c)
    ynbr = seq_of(1 - y, x, c)
    xl, xr, xd = (x + 3) % 4, (x + 1) % 4, (x + 2) % 4
    left, right = seq_of(y, xl, c), seq_of(y, xr, c)
    xnbr = seq_of(y, (x + 3 + 2 * c) % 4, 1 - c)
    slots = {"O": chip, "Y": (1 - y) * 4 + x, "L": y * 4 + xl, "R": y * 4 + xr,
             "LY": (1 - y) * 4 + xl, "RY": (1 - y) * 4 + xr,
             "D": y * 4 + xd, "DY": (1 - y) * 4 + xd}
    up, dn, hn = yh * 4 + (z + 1) % 4, yh * 4 + (z + 3) % 4, (1 - yh) * 4 + z
    places = {"O": h, "Up": up, "Dn": dn, "H": hn,
              "HUp": (1 - yh) * 4 + (z + 1) % 4, "HDn": (1 - yh) * 4 + (z + 3) % 4,
              "D2": yh * 4 + (z + 2) % 4, "HD2": (1 - yh) * 4 + (z + 2) % 4}
    home = jnp.where(h == s // 2, 1, 0)

    barrier = pltpu.get_barrier_semaphore()

    def greet(d, carry):
        pl.semaphore_signal(barrier, inc=1, device_id={"seq": (s + d) % 16}, device_id_type=MESH)
        return carry

    lax.fori_loop(1, 16, greet, 0)
    for peer in (up, dn, hn):
        pl.semaphore_signal(barrier, inc=1, device_id={"head": peer}, device_id_type=MESH)

    def greet_far(i, carry):
        far_s, far_h = 2 * h + i % 2, i // 2

        @pl.when(jnp.logical_or(far_s != s, far_h != h))
        def _():
            pl.semaphore_signal(barrier, inc=1, device_id={"seq": far_s, "head": far_h},
                                device_id_type=MESH)
        return carry

    lax.fori_loop(0, 16, greet_far, 0)
    pl.semaphore_wait(barrier, 15 + 3 + 16 - home)

    sent = []

    class Gather:
        def __init__(self, buf, ssem, rsem, cut):
            self.buf, self.ssem, self.rsem, self.cut = buf, ssem, rsem, cut

        def view(self, place, core, half):
            ref = self.buf.at[slots[place], core]
            if half == "":
                return ref
            return ref.at[pl.ds(0 if half == "a" else self.cut, self.cut)]

        def push(self, place, core, half, kind, to, src=None):
            ref = self.view(place, core, half)
            cp = remote(ref if src is None else src, ref, self.ssem.at[GID[kind]],
                        self.rsem.at[GID[kind]], to)
            cp.start()
            sent.append(cp)

        def arrive(self, place, core, half, kind):
            ref = self.view(place, core, half)
            remote(ref, ref, self.ssem.at[GID[kind]], self.rsem.at[GID[kind]], partner).wait_recv()

    wg = Gather(wbuf, send, recv, SHARD // 2)
    pg = Gather(wp, psend, precv, 4)

    wg.push("O", c, "", "Y", ynbr, src=w)
    wg.push("O", c, "", "L", right, src=w)
    wg.push("O", c, "", "R", left, src=w)
    wg.push("O", c, "", "PO", partner, src=w)
    keep = pltpu.make_async_copy(w, wbuf.at[chip, c], own_sem.at[0])
    keep.start()

    def layer_norm(vals, shift, scale):
        vals = vals.astype(F32)
        vals = vals - jnp.mean(vals, axis=1, keepdims=True)
        spread = jnp.mean(jnp.square(vals), axis=1, keepdims=True)
        return (vals * lax.rsqrt(spread + 1e-6) * scale + shift).astype(BF)

    text_normed = layer_norm(txt[...], modt[pl.ds(0, 1), :], 1.0 + modt[pl.ds(1, 1), :])
    for d in range(16):
        nt[d] = text_normed[:, d * SHARD:(d + 1) * SHARD]
    own_row = c * 8 + chip

    def scatter(d, carry):
        to = (s + d) % 16
        remote(nt.at[to], tnt.at[own_row], tsend.at[d], trecv.at[d], to).start()
        return carry

    lax.fori_loop(1, 16, scatter, 0)
    keep_t = pltpu.make_async_copy(nt.at[s], tnt.at[own_row], own_sem.at[1])
    keep_t.start()

    def pieces(j, carry):
        to_s, to_h = 2 * j + c, s // 2
        here = jnp.logical_and(to_s == s, to_h == h)

        @pl.when(jnp.logical_not(here))
        def _():
            remote(pv.at[:, j], wp.at[j, c, h], wsend.at[j], wrecv.at[h], to_s, to_h).start()

        @pl.when(here)
        def _():
            pltpu.make_async_copy(pv.at[:, j], wp.at[j, c, h], own_sem.at[2]).start()
        return carry

    lax.fori_loop(0, 8, pieces, 0)

    shift = modv[pl.ds(0, 1), :]
    scale = 1.0 + modv[pl.ds(1, 1), :]

    def norm_rows(i, carry):
        to = (i % TILES) * 8 + i // TILES
        normed[pl.ds(pl.multiple_of(to * 16, 16), 16), :] = layer_norm(
            vid[pl.ds(pl.multiple_of(i * 16, 16), 16), :], shift, scale)
        return carry

    lax.fori_loop(0, 40, norm_rows, 0)

    def scattered(d, carry):
        remote(nt.at[0], tnt.at[0], tsend.at[d], trecv.at[d], partner).wait_recv()
        return carry

    lax.fori_loop(1, 16, scattered, 0)
    keep_t.wait()
    for g in range(3):
        cols = pl.ds(g * PART, PART)
        part[:, :, :, cols] = jnp.dot(
            tnt[...].reshape(256, SHARD), wt[:, cols], preferred_element_type=F32
        ).reshape(2, 8, 16, PART)
    swap = remote(part.at[1 - c], ppart, rsend.at[0], rrecv.at[0], partner)
    swap.start()

    wg.arrive("L", c, "", "L")
    wg.push("L", c, "a", "Da", right)
    wg.arrive("R", c, "", "R")
    wg.push("R", c, "b", "Db", left)
    wg.arrive("Y", c, "", "Y")
    wg.push("Y", c, "", "RY", left)
    wg.push("Y", c, "", "LY", right)
    wg.push("L", c, "", "PL", partner)
    wg.push("R", c, "", "PR", partner)
    wg.push("Y", c, "", "PY", partner)

    swap.wait()
    part[pl.ds(c, 1)] = part[pl.ds(c, 1)] + ppart[...].reshape(1, 8, 16, WIDE)

    def reduce_send(d, carry):
        j = (chip + d) % 8
        remote(part.at[c, j], tsum_in.at[d], rsend.at[d], rrecv.at[d], 2 * j + c).start()
        return carry

    lax.fori_loop(1, 8, reduce_send, 0)

    def multiply(place, first=False):
        j = slots[place]
        lhs = normed[:, pl.ds(pl.multiple_of(j * PART, PART), PART)]
        for g in range(3):
            cols = pl.ds(g * PART, PART)
            term = jnp.dot(lhs, wbuf[j, :, :, cols].reshape(PART, PART), preferred_element_type=F32)
            if first:
                acc[:, cols] = term
            else:
                acc[:, cols] += term

    keep.wait()
    wg.arrive("O", 1 - c, "", "PO")
    multiply("O", True)
    wg.arrive("Y", 1 - c, "", "PY")
    multiply("Y")
    wg.arrive("L", 1 - c, "", "PL")
    multiply("L")
    wg.arrive("D", c, "a", "Da")
    wg.push("D", c, "a", "DYa", ynbr)
    wg.push("D", c, "a", "PDa", partner)
    wg.arrive("D", c, "b", "Db")
    wg.push("D", c, "b", "DYb", ynbr)
    wg.push("D", c, "b", "PDb", partner)
    wg.arrive("R", 1 - c, "", "PR")
    multiply("R")
    wg.arrive("LY", c, "", "LY")
    wg.push("LY", c, "", "PLY", partner)
    wg.arrive("RY", c, "", "RY")
    wg.push("RY", c, "", "PRY", partner)
    wg.arrive("D", 1 - c, "a", "PDa")
    wg.arrive("D", 1 - c, "b", "PDb")
    multiply("D")
    wg.arrive("DY", c, "a", "DYa")
    wg.push("DY", c, "a", "PDYa", partner)
    wg.arrive("LY", 1 - c, "", "PLY")
    multiply("LY")
    wg.arrive("DY", c, "b", "DYb")
    wg.push("DY", c, "b", "PDYb", partner)
    wg.arrive("RY", 1 - c, "", "PRY")
    multiply("RY")
    wg.arrive("DY", 1 - c, "a", "PDYa")
    wg.arrive("DY", 1 - c, "b", "PDYb")
    multiply("DY")

    def kv_push(k, n, to, src=None):
        src = kv.at[n] if src is None else src
        cp = remote(src, kvbuf.at[k, n], ksend.at[k, n], krecv.at[k, n], to)
        cp.start()
        sent.append(cp)

    def kv_arrive(k, n):
        ref = kvbuf.at[k, n]
        remote(ref, ref, ksend.at[k, n], krecv.at[k, n], partner).wait_recv()

    for n in range(3):
        def finish(i, carry, n=n):
            rows = pl.ds(pl.multiple_of(i * 128, 128), 128)
            kv[n, rows, :HD] = head_normed(
                acc[rows, PART + n * HD:PART + (n + 1) * HD], gainv[pl.ds(1, 1), :]).astype(BF)
            kv[n, rows, HD:] = acc[rows, 2 * PART + n * HD:2 * PART + (n + 1) * HD].astype(BF)
            return carry

        lax.fori_loop(0, TILES, finish, 0)
        kv_push(1, n, ynbr)
        if n < 2:
            kv_push(3, n, xnbr)
        kv_push(0, n, partner)

    def finish_q(i, carry):
        rows = pl.ds(pl.multiple_of(i * 128, 128), 128)
        for n in range(3):
            q[n, rows] = head_normed(acc[rows, n * HD:(n + 1) * HD], gainv[pl.ds(0, 1), :]).astype(BF)
        return carry

    lax.fori_loop(0, TILES, finish_q, 0)

    def reduced(d, carry):
        remote(part.at[0, 0], tsum_in.at[d], rsend.at[d], rrecv.at[d], partner).wait_recv()
        return carry

    lax.fori_loop(1, 8, reduced, 0)
    total = part[pl.ds(c, 1), pl.ds(chip, 1)].reshape(16, WIDE)
    for d in range(1, 8):
        total = total + tsum_in[d]
    for n in range(6):
        hd = total[:, n * HD:(n + 1) * HD]
        tall[pl.ds(s, 1), :, n * HD:(n + 1) * HD] = head_normed(
            hd, gaint[pl.ds(n // 3, 1), :]).astype(BF).reshape(1, 16, HD)
    tall[pl.ds(s, 1), :, 768:] = total[:, 768:].astype(BF).reshape(1, 16, PART)

    def give(d, carry):
        j = (chip + d) % 8
        remote(tall.at[s], tall.at[s], gsend.at[d], grecv.at[d], 2 * j + c).start()
        return carry

    lax.fori_loop(1, 8, give, 0)
    remote(tall.at[s], tall.at[s], gsend.at[0], grecv.at[0], partner).start()

    height = 2 * x + c
    x_there = jnp.where(jnp.logical_or(jnp.logical_and(height == 0, c == 0),
                                       jnp.logical_and(height == 7, c == 1)), 0, 1)
    lane_tile = lax.broadcasted_iota(jnp.int32, (1, ROWS), 1) // 128

    def attend(n, keys, values, bias_of, first=False):
        def tile(i, carry):
            rows = pl.ds(pl.multiple_of(i * 128, 128), 128)
            t = lax.dot_general(q[n, rows], keys(), (((1,), (1,)), ((), ())),
                                preferred_element_type=F32) * SCALE2 + bias_of(i)
            peak = jnp.max(t, axis=1, keepdims=True)
            if first:
                new = peak
            else:
                old = top[n, rows, :]
                new = jnp.maximum(old, peak)
            p = jnp.exp2(t - new[:, :1]).astype(BF)
            gain = jnp.dot(p, with_ones(values()), preferred_element_type=F32)
            if first:
                att[n, rows, :] = gain
            else:
                factor = jnp.exp2(old - new)
                att[n, rows, :] = att[n, rows, :] * jnp.concatenate([factor, factor], axis=1) + gain
            top[n, rows, :] = jnp.broadcast_to(new, (128, HD))
            return carry

        lax.fori_loop(0, TILES, tile, 0)

    def window_bias(n, dt, dh, there):
        row = h * 3 + n
        fits = jnp.logical_and(windows[row, 0] >= dt, windows[row, 1] >= dh)
        reach = jnp.where(fits, windows[row, 2], -1)
        if there is not None:
            reach = jnp.where(there == 1, reach, -1)
        return lambda i: jnp.where(jnp.abs(lane_tile - i) <= reach, 0.0, NEG_BIG)

    def attend_block(k, n):
        dt = 1 if k in (1, 2, 4) else 0
        dh = 1 if k in (0, 2, 3, 4) else 0
        there = x_there if k in (3, 4) else None
        attend(n, lambda: kvbuf[k, n, :, :HD], lambda: kvbuf[k, n, :, HD:], window_bias(n, dt, dh, there))

    for n in range(3):
        attend(n, lambda n=n: kv[n, :, :HD], lambda n=n: kv[n, :, HD:], window_bias(n, 0, 0, None), True)

    for d in range(1, 8):
        j = (chip + 8 - d) % 8
        block = tall.at[2 * j + c]
        remote(block, block, gsend.at[d], grecv.at[d], partner).wait_recv()
        remote(block, block, gsend.at[7 + d], grecv.at[7 + d], partner).start()
    for n in range(3):
        kv_arrive(0, n)
        attend_block(0, n)
    for d in range(1, 8):
        j = (chip + 8 - d) % 8
        block = tall.at[2 * j + 1 - c]
        remote(block, block, gsend.at[7 + d], grecv.at[7 + d], partner).wait_recv()
    block = tall.at[partner]
    remote(block, block, gsend.at[0], grecv.at[0], partner).wait_recv()

    def text_cols(g, n):
        return tall[:, :, g * PART + n * HD:g * PART + (n + 1) * HD].reshape(256, HD)

    lane = lax.broadcasted_iota(jnp.int32, (16, HD), 1)

    def text_part(i, carry):
        blocks = pl.ds(i * 8, 8)
        stat = jnp.zeros((128, HD), F32)
        lanes = lax.broadcasted_iota(jnp.int32, (128, HD), 1)
        for n in range(3):
            tq = tall[blocks, :, n * HD:(n + 1) * HD].reshape(128, HD)
            t = lax.dot_general(tq, kv[n, :, :HD], (((1,), (1,)), ((), ())),
                                preferred_element_type=F32) * SCALE2
            peak = jnp.max(t, axis=1, keepdims=True)
            p = jnp.exp2(t - peak).astype(BF)
            both = jnp.dot(p, with_ones(kv[n, :, HD:]), preferred_element_type=F32)
            ts[blocks, :, n * HD:(n + 1) * HD] = (both[:, :HD] / both[:, HD:]).reshape(8, 16, HD)
            stat = jnp.where(lanes == n, peak + jnp.log2(both[:, HD:]), stat)
        ts[blocks, :, PART:] = stat.reshape(8, 16, HD)
        return carry

    lax.fori_loop(0, 2, text_part, 0)

    def merge_send(d, carry):
        to = (s + d) % 16
        remote(ts.at[to], ts_in.at[d], msend.at[d], mrecv.at[d], to).start()
        return carry

    lax.fori_loop(1, 16, merge_send, 0)

    text_row = jnp.where(lax.broadcasted_iota(jnp.int32, (1, 256), 1) < text_len[0], 0.0, NEG_BIG)

    def attend_text(n):
        attend(n, lambda: text_cols(1, n), lambda: text_cols(2, n), lambda i: text_row)

    def ring_push(place, n, half, kind, to):
        ref = attbuf.at[places[place], n]
        if half:
            ref = ref.at[pl.ds(0 if half == "a" else ROWS // 2, ROWS // 2)]
        cp = remote(ref, ref, zsend.at[RID[kind], n], zrecv.at[RID[kind], n], None, to)
        cp.start()
        sent.append(cp)

    def ring_arrive(place, n, half, kind):
        ref = attbuf.at[places[place], n]
        if half:
            ref = ref.at[pl.ds(0 if half == "a" else ROWS // 2, ROWS // 2)]
        remote(ref, ref, zsend.at[RID[kind], n], zrecv.at[RID[kind], n], None, up).wait_recv()

    def close_head(n):
        def tile(i, carry):
            rows = pl.ds(pl.multiple_of(i * 128, 128), 128)
            attbuf[pl.ds(h, 1), n, rows, :] = (
                att[n, rows, :HD] / att[n, rows, HD:]).astype(BF).reshape(1, 128, HD)
            return carry

        lax.fori_loop(0, TILES, tile, 0)
        ring_push("O", n, "", "H", hn)
        ring_push("O", n, "", "Dn", up)
        ring_push("O", n, "", "Up", dn)

    def ring_one(n):
        ring_arrive("H", n, "", "H")
        ring_push("H", n, "", "HDn", up)
        ring_push("H", n, "", "HUp", dn)
        ring_arrive("Dn", n, "", "Dn")
        ring_push("Dn", n, "a", "D2a", up)
        ring_arrive("Up", n, "", "Up")
        ring_push("Up", n, "b", "D2b", dn)

    def ring_two(n):
        ring_arrive("HDn", n, "", "HDn")
        ring_push("HDn", n, "a", "HD2a", up)
        ring_arrive("HUp", n, "", "HUp")
        ring_push("HUp", n, "b", "HD2b", dn)

    def ring_three(n):
        for half in ("a", "b"):
            ring_arrive("D2", n, half, "D2" + half)
            ring_arrive("HD2", n, half, "HD2" + half)

    def project(n, first=False):
        def one(j, carry):
            rhs = jnp.concatenate(
                [wp[:, 0, j, n].reshape(HD, SHARD), wp[:, 1, j, n].reshape(HD, SHARD)], axis=1)
            acc2[...] += jnp.dot(attbuf[j, n], rhs, preferred_element_type=F32)
            return carry

        lax.fori_loop(0, 8, one, 0)

    kv_arrive(1, 0)
    kv_push(4, 0, xnbr, kvbuf.at[1, 0])
    kv_push(3, 2, xnbr)
    kv_push(2, 0, partner, kvbuf.at[1, 0])
    attend_text(0)
    attend_block(1, 0)
    kv_arrive(2, 0)
    attend_block(2, 0)
    kv_arrive(3, 0)
    attend_block(3, 0)
    attend_text(1)
    attend_text(2)
    kv_arrive(4, 0)
    attend_block(4, 0)
    close_head(0)

    kv_arrive(1, 1)
    kv_push(4, 1, xnbr, kvbuf.at[1, 1])
    kv_push(2, 1, partner, kvbuf.at[1, 1])
    attend_block(1, 1)
    kv_arrive(2, 1)
    attend_block(2, 1)
    kv_arrive(3, 1)
    attend_block(3, 1)
    ring_one(0)

    def piece(j, carry):
        @pl.when(jnp.logical_not(jnp.logical_and(s // 2 == h, j == h)))
        def _():
            remote(wp.at[0, 0, 0], wp.at[chip, c, j], wsend.at[0], wrecv.at[j], partner).wait_recv()
        return carry

    lax.fori_loop(0, 8, piece, 0)

    @pl.when(home == 1)
    def _():
        pltpu.make_async_copy(pv.at[:, 0], wp.at[chip, c, h], own_sem.at[2]).wait()

    pg.push("O", c, "", "Y", ynbr)
    pg.push("O", c, "", "L", right)
    pg.push("O", c, "", "R", left)
    pg.push("O", c, "", "PO", partner)

    kv_arrive(4, 1)
    attend_block(4, 1)
    close_head(1)
    ring_two(0)

    kv_arrive(1, 2)
    kv_push(4, 2, xnbr, kvbuf.at[1, 2])
    kv_push(2, 2, partner, kvbuf.at[1, 2])
    attend_block(1, 2)
    kv_arrive(2, 2)
    attend_block(2, 2)
    kv_arrive(3, 2)
    attend_block(3, 2)
    ring_one(1)

    def merge_wait(d, carry):
        remote(ts.at[0], ts_in.at[d], msend.at[d], mrecv.at[d], partner).wait_recv()
        return carry

    lax.fori_loop(1, 16, merge_wait, 0)
    ts_in[0] = ts[pl.ds(s, 1)].reshape(16, 512)
    for n in range(3):
        tq = tall[pl.ds(s, 1), :, n * HD:(n + 1) * HD].reshape(16, HD)
        t = lax.dot_general(tq, text_cols(1, n), (((1,), (1,)), ((), ())),
                            preferred_element_type=F32) * SCALE2 + text_row
        peak = jnp.max(t, axis=1, keepdims=True)
        p = jnp.exp2(t - peak).astype(BF)
        both = jnp.dot(p, with_ones(text_cols(2, n)), preferred_element_type=F32)
        logs = [ts_in[d, :, PART + n:PART + n + 1] for d in range(16)]
        high = peak + jnp.log2(both[:, HD:HD + 1])
        for value in logs:
            high = jnp.maximum(high, value)
        weight = jnp.exp2(peak - high)
        upper = both[:, :HD] * weight
        lower = both[:, HD:HD + 1] * weight
        for d in range(16):
            weight = jnp.exp2(logs[d] - high)
            upper = upper + ts_in[d, :, n * HD:(n + 1) * HD] * weight
            lower = lower + weight
        atg[pl.ds(s, 1), :, n * HD:(n + 1) * HD] = (upper / lower).astype(BF).reshape(1, 16, HD)

    def text_give(d, carry):
        remote(atg.at[s], atg.at[s], asend.at[d], arecv.at[d], (s + d) % 16).start()
        return carry

    lax.fori_loop(1, 16, text_give, 0)

    pg.arrive("L", c, "", "L")
    pg.push("L", c, "a", "Da", right)
    pg.arrive("R", c, "", "R")
    pg.push("R", c, "b", "Db", left)
    pg.arrive("Y", c, "", "Y")
    pg.push("Y", c, "", "RY", left)
    pg.push("Y", c, "", "LY", right)
    pg.push("L", c, "", "PL", partner)
    pg.push("R", c, "", "PR", partner)
    pg.push("Y", c, "", "PY", partner)

    kv_arrive(4, 2)
    attend_block(4, 2)
    close_head(2)
    ring_two(1)

    pg.arrive("D", c, "a", "Da")
    pg.push("D", c, "a", "DYa", ynbr)
    pg.push("D", c, "a", "PDa", partner)
    pg.arrive("D", c, "b", "Db")
    pg.push("D", c, "b", "DYb", ynbr)
    pg.push("D", c, "b", "PDb", partner)
    pg.arrive("LY", c, "", "LY")
    pg.push("LY", c, "", "PLY", partner)
    pg.arrive("RY", c, "", "RY")
    pg.push("RY", c, "", "PRY", partner)

    def text_given(d, carry):
        block = atg.at[(s + 16 - d) % 16]
        remote(block, block, asend.at[d], arecv.at[d], partner).wait_recv()
        return carry

    lax.fori_loop(1, 16, text_given, 0)
    tpart[...] = jnp.dot(atg[...].reshape(256, PART), pt[...],
                         preferred_element_type=F32).reshape(16, 16, SHARD)

    def text_move(i, carry):
        here = jnp.logical_and(i == s, s // 2 == h)

        @pl.when(jnp.logical_not(here))
        def _():
            remote(tpart.at[i], tpart_in.at[c, h], osend.at[i], orecv.at[c, h], i, s // 2).start()

        @pl.when(here)
        def _():
            pltpu.make_async_copy(tpart.at[i], tpart_in.at[c, h], own_sem.at[3]).start()
        return carry

    lax.fori_loop(0, 16, text_move, 0)

    ring_one(2)
    pg.arrive("DY", c, "a", "DYa")
    pg.push("DY", c, "a", "PDYa", partner)
    pg.arrive("DY", c, "b", "DYb")
    pg.push("DY", c, "b", "PDYb", partner)
    pg.arrive("O", 1 - c, "", "PO")
    for place in ("Y", "L", "R", "LY", "RY"):
        pg.arrive(place, 1 - c, "", "P" + place)
    for half in ("a", "b"):
        pg.arrive("D", 1 - c, half, "PD" + half)
        pg.arrive("DY", 1 - c, half, "PDY" + half)
    acc2[...] = jnp.zeros_like(acc2)
    ring_three(0)
    project(0)
    ring_two(2)
    ring_three(1)
    project(1)

    def text_moved(i, carry):
        @pl.when(jnp.logical_not(jnp.logical_and(2 * h + i % 2 == s, i // 2 == h)))
        def _():
            remote(tpart.at[0], tpart_in.at[i % 2, i // 2], osend.at[0], orecv.at[i % 2, i // 2],
                   partner).wait_recv()
        return carry

    lax.fori_loop(0, 16, text_moved, 0)

    @pl.when(home == 1)
    def _():
        pltpu.make_async_copy(tpart.at[0], tpart_in.at[c, h], own_sem.at[3]).wait()

    out_cols = pl.ds(pl.multiple_of(h * PART, PART), PART)
    sums = jnp.concatenate([jnp.sum(tpart_in[0], axis=0), jnp.sum(tpart_in[1], axis=0)], axis=1)
    text_out[...] = (txt[:, out_cols].astype(F32) + modt[pl.ds(2, 1), out_cols] * sums).astype(BF)

    ring_three(2)
    project(2)
    gate = modv[pl.ds(2, 1), out_cols]

    def write(i, carry):
        rows = pl.ds(pl.multiple_of(i * 16, 16), 16)
        at = pl.ds(pl.multiple_of(((i % TILES) * 8 + i // TILES) * 16, 16), 16)
        video_out[rows, :] = (vid[rows, out_cols].astype(F32) + gate * acc2[at, :]).astype(BF)
        return carry

    lax.fori_loop(0, 40, write, 0)

    def left_t(d, carry):
        remote(nt.at[0], tnt.at[0], tsend.at[d], trecv.at[d], partner).wait_send()
        remote(ts.at[0], ts_in.at[0], msend.at[d], mrecv.at[d], partner).wait_send()
        remote(atg.at[0], atg.at[0], asend.at[d], arecv.at[d], partner).wait_send()
        return carry

    lax.fori_loop(1, 16, left_t, 0)

    def left_r(d, carry):
        remote(part.at[0, 0], tsum_in.at[d], rsend.at[d], rrecv.at[d], partner).wait_send()
        return carry

    lax.fori_loop(1, 8, left_r, 0)

    def left_g(d, carry):
        remote(tall.at[0], tall.at[0], gsend.at[d], grecv.at[d], partner).wait_send()
        return carry

    lax.fori_loop(0, 15, left_g, 0)

    def left_w(j, carry):
        @pl.when(jnp.logical_not(jnp.logical_and(2 * j + c == s, s // 2 == h)))
        def _():
            remote(pv.at[:, 0], wp.at[0, 0, 0], wsend.at[j], wrecv.at[0], partner).wait_send()
        return carry

    lax.fori_loop(0, 8, left_w, 0)

    def left_o(i, carry):
        @pl.when(jnp.logical_not(jnp.logical_and(i == s, s // 2 == h)))
        def _():
            remote(tpart.at[0], tpart_in.at[0, 0], osend.at[i], orecv.at[0, 0], partner).wait_send()
        return carry

    lax.fori_loop(0, 16, left_o, 0)
    for cp in sent:
        cp.wait_send()


def block_kernel(vid, txt, modv, modt, w, wt, pv, pt, gainv, gaint, windows, text_len):
    vm = pl.BlockSpec(memory_space=pltpu.VMEM)
    sm = pl.BlockSpec(memory_space=pltpu.SMEM)
    dma = pltpu.SemaphoreType.DMA
    v = pltpu.VMEM
    return pl.pallas_call(
        kernel,
        name="attention_block",
        out_shape=(jax.ShapeDtypeStruct((ROWS, PART), BF), jax.ShapeDtypeStruct((16, PART), BF)),
        in_specs=[vm] * 10 + [sm, sm],
        out_specs=(vm, vm),
        scratch_shapes=[
            v((ROWS, 3072), BF), v((8, 2, SHARD, WIDE), BF), v((ROWS, WIDE), F32),
            v((16, 16, SHARD), BF), v((16, 16, SHARD), BF),
            v((2, 8, 16, WIDE), F32), v((8, 16, WIDE), F32), v((8, 16, WIDE), F32),
            v((16, 16, WIDE), BF),
            v((3, ROWS, HD), BF), v((3, ROWS, 2 * HD), BF), v((5, 3, ROWS, 2 * HD), BF),
            v((3, ROWS, HD), F32), v((3, ROWS, 2 * HD), F32), v((8, 3, ROWS, HD), BF),
            v((8, 2, 8, 3, 16, SHARD), BF), v((ROWS, PART), F32),
            v((16, 16, 512), F32), v((16, 16, 512), F32), v((16, 16, PART), BF),
            v((16, 16, SHARD), F32), v((2, 8, 16, SHARD), F32),
            dma((4,)), dma((19,)), dma((19,)), dma((16,)), dma((16,)),
            dma((8,)), dma((8,)), dma((15,)), dma((15,)),
            dma((5, 3)), dma((5, 3)), dma((9, 3)), dma((9, 3)),
            dma((8,)), dma((8,)), dma((19,)), dma((19,)),
            dma((16,)), dma((16,)), dma((16,)), dma((16,)), dma((16,)), dma((2, 8)),
        ],
        compiler_params=pltpu.CompilerParams(
            collective_id=1, has_side_effects=True, vmem_limit_bytes=58 * 2**20),
    )(vid, txt, modv, modt, w, wt, pv, pt, gainv, gaint, windows, text_len)


def body(video_in, text_in, mod_video, mod_text, qkv_video, qkv_text, proj_video, proj_text,
         gain_video, gain_text, windows, text_len):
    return block_kernel(
        video_in, text_in, mod_video, mod_text,
        qkv_video.reshape(SHARD, WIDE), qkv_text.reshape(SHARD, WIDE),
        proj_video.reshape(3, 8, 16, SHARD), proj_text,
        gain_video, gain_text, windows, text_len)


def solution(mesh):
    return jax.shard_map(
        body,
        mesh=mesh,
        in_specs=(
            P("seq", None), P("seq", None), P(), P(),
            P("seq", None, "head"), P("seq", None, "head"),
            P("head", "seq"), P("head", "seq"), P(), P(), P(), P(),
        ),
        out_specs=(P("seq", "head"), P("seq", "head")),
        check_vma=False,
    )
```

time: 688 us -> 179 us (0.26)
  waiting for transfers between devices: 279 us -> 0 us
  Pallas kernels: 0 us -> 166 us
  blocking collectives: 118 us -> 0 us
  matrix products: 106 us -> 0 us
  other arithmetic: 84 us -> 0 us
  local copies, waits for them, and re-layouts: 57.1 us -> 11.6 us
  starting transfers between devices: 19.1 us -> 0 us
  between operations: 15.4 us -> 1.29 us
    pallas_call x0 -> x1, Pallas kernels: none -> 166 us  [block_kernel(): pl.pallas_call(kernel, name='attention_block', out_shape=(jax.ShapeDtypeS...]
    all_gather x5 -> x0, waiting for transfers between devices: 141 us -> none  [the longest x1 44.4 us: body(): lax.all_gather(qkv_video, 'seq', axis=0, tiled=True)]
    all_gather x5 -> x0, blocking collectives: 118 us -> none  [the longest x1 37.6 us: body(): lax.all_gather(key_t, 'seq', axis=0, tiled=True)]
    dot_general x28 -> x0, matrix products: 106 us -> none  [the longest x12 57.5 us: attend_block(): jnp.einsum('qhd,khd->hqk', queries, key_vecs, preferred_element_type=jnp....]
    unnamed x9 -> x0, waiting for transfers between devices: 92.2 us -> none
    ppermute x8 -> x0, waiting for transfers between devices: 46.1 us -> none  [passed_along(): return lax.ppermute(shard, axis, pairs)]
    reduce_sum x20 -> x0, other arithmetic: 45.6 us -> none  [the longest x12 39 us: attend_block(): row_sum = row_sum * factor + jnp.sum(powers, axis=2)]
    add x50 -> x0, other arithmetic: 21.2 us -> none  [the longest x15 20.4 us: combine(): earlier[2] * weight_one[:, :, None] + later[2] * weight_two[:, :, None]]
  transfers between devices with their start and end apart: 15 -> 0, of which waited for: 8 -> 0; matrix products, arithmetic and copies ran while one was open for 31% -> 0% of each run, Pallas kernels for 0% -> 0%
where the time goes in v1:
time: 179 us
  Pallas kernels  166 us (93%)
  local copies, waits for them, and re-layouts  11.6 us (6%)
    pallas_call x1, Pallas kernels, block_kernel(): pl.pallas_call(kernel, name='attention_block', out_shape=(jax.ShapeDtypeS...  166 us
    unnamed x5, local copies, waits for them, and re-layouts  7.98 us

profile of v1, /device:TPU:1, one launch (start us, length us, event | category | flops | bytes accessed | tf_op | source)
XLA Modules:
  0.0 178.8 jit_solution(9676054575477294492)
XLA Ops:
  1.3 1.4 copy.23.windows
  2.6 1.7 copy.21
  4.4 1.7 copy.22.pt
  6.1 1.8 %copy.24 = bf16[3,24,8,384]{3,2,0,1:T(8,128)(2,1)} copy(bf16[3,24,8,384]{3,2,1,0:T(8,128)(2,1)} %bitcast.8) | data formatting | bytes 884736 | tf_op jit(solution)/shard_map/reshape | solution.py:726
  7.9 1.8 %copy.25 = bf16[3,24,8,384]{3,2,0,1:T(8,128)(2,1)} copy(bf16[3,24,8,384]{3,2,1,0:T(8,128)(2,1)} %bitcast.9) | data formatting | bytes 884736 | tf_op jit(solution)/shard_map/reshape | solution.py:726
  9.7 165.8 %attention_block.1 = (bf16[640,384]{1,0:T(8,128)(2,1)}, bf16[16,384]{1,0:T(8,128)(2,1)}) custom-call(bf16[640,3072]{1,0:T(8,128)(2,1)} %vid.1, bf16[16,3072]{1,0:T(8,128)(2,1)} %txt.1, f32[3,3072]{1,0:T(4,128)} %modv.1, f32[3,3072]{1,0:T(4,128)} %modt.1, bf16[192,1152]{1,0:T(8,128)(2,1)} %bitcast.5, bf16[192,1152]{1,0:T(8,128)(2,1)} %bitcast.6, ...), custom_call_target="tpu_custom_call" | custom-call | tf_op jit(solution)/shard_map/attention_block/pallas_call | solution.py:695
  175.6 1.9 %copy.29 = bf16[640,384]{1,0:T(8,128)(2,1)} copy(bf16[640,384]{1,0:T(8,128)(2,1)} %get-tuple-element.4) | data formatting | bytes 983040
  177.5 1.3 copy.30

commit v2 on v1

--- a/solution.py
+++ b/solution.py
@@ -45,9 +45,9 @@
     return jnp.concatenate([value, jnp.ones_like(value)], axis=1)
 
 
-def kernel(vid, txt, modv, modt, w, wt, pv, pt, gainv, gaint, windows, text_len,
+def kernel(vid_hbm, txt, modv, modt, w, wt_hbm, pv_hbm, pt_hbm, gainv, gaint, windows, text_len,
            video_out, text_out,
-           normed, wbuf, acc, nt, tnt, part, ppart, tsum_in, tall,
+           vid, wt, pvt, pt, pv, normed, wbuf, acc, nt, tnt, part, ppart, tsum_in, tall,
            q, kv, kvbuf, top, att, attbuf, wp, acc2,
            ts, ts_in, atg, tpart, tpart_in,
            own_sem, send, recv, tsend, trecv, rsend, rrecv, gsend, grecv,
@@ -76,6 +76,20 @@
               "D2": yh * 4 + (z + 2) % 4, "HD2": (1 - yh) * 4 + (z + 2) % 4}
     home = jnp.where(h == s // 2, 1, 0)
 
+    def fetch(i, src, dst):
+        cp = pltpu.make_async_copy(src, dst, own_sem.at[i])
+        cp.start()
+        return cp
+
+    def shard(n):
+        return w.at[:, :, pl.ds(n * HD, HD)]
+
+    fetch_vid = fetch(4, vid_hbm, vid)
+    fetch_pv = fetch(5, pv_hbm, pvt)
+    fetch_wt = fetch(6, wt_hbm, wt)
+    fetch_pt = fetch(7, pt_hbm, pt)
+    keep = [fetch(8 + n, shard(n), wbuf.at[n, chip, c]) for n in range(3)]
+
     barrier = pltpu.get_barrier_semaphore()
 
     def greet(d, carry):
@@ -101,14 +115,12 @@
     sent = []
 
     class Gather:
-        def __init__(self, buf, ssem, rsem, cut):
-            self.buf, self.ssem, self.rsem, self.cut = buf, ssem, rsem, cut
+        def __init__(self, at, ssem, rsem, cut):
+            self.at, self.ssem, self.rsem, self.cut = at, ssem, rsem, cut
 
         def view(self, place, core, half):
-            ref = self.buf.at[slots[place], core]
-            if half == "":
-                return ref
-            return ref.at[pl.ds(0 if half == "a" else self.cut, self.cut)]
+            ref = self.at(slots[place], core)
+            return self.cut(ref, half) if half else ref
 
         def push(self, place, core, half, kind, to, src=None):
             ref = self.view(place, core, half)
@@ -121,15 +133,57 @@
             ref = self.view(place, core, half)
             remote(ref, ref, self.ssem.at[GID[kind]], self.rsem.at[GID[kind]], partner).wait_recv()
 
-    wg = Gather(wbuf, send, recv, SHARD // 2)
-    pg = Gather(wp, psend, precv, 4)
-
-    wg.push("O", c, "", "Y", ynbr, src=w)
-    wg.push("O", c, "", "L", right, src=w)
-    wg.push("O", c, "", "R", left, src=w)
-    wg.push("O", c, "", "PO", partner, src=w)
-    keep = pltpu.make_async_copy(w, wbuf.at[chip, c], own_sem.at[0])
-    keep.start()
+        def own(self, src=None):
+            self.push("O", c, "", "L", right, src)
+            self.push("O", c, "", "R", left, src)
+            self.push("O", c, "", "Y", ynbr, src)
+            self.push("O", c, "", "PO", partner, src)
+
+        def one(self):
+            self.arrive("L", c, "", "L")
+            self.push("L", c, "a", "Da", right)
+            self.arrive("R", c, "", "R")
+            self.push("R", c, "b", "Db", left)
+            self.arrive("Y", c, "", "Y")
+            self.push("Y", c, "", "RY", left)
+            self.push("Y", c, "", "LY", right)
+            self.push("L", c, "", "PL", partner)
+            self.push("R", c, "", "PR", partner)
+            self.push("Y", c, "", "PY", partner)
+
+        def two(self):
+            for half in ("a", "b"):
+                self.arrive("D", c, half, "D" + half)
+                self.push("D", c, half, "DY" + half, ynbr)
+                self.push("D", c, half, "PD" + half, partner)
+            for place in ("LY", "RY"):
+                self.arrive(place, c, "", place)
+                self.push(place, c, "", "P" + place, partner)
+
+        def three(self):
+            for half in ("a", "b"):
+                self.arrive("DY", c, half, "DY" + half)
+                self.push("DY", c, half, "PDY" + half, partner)
+
+        def pair(self, place):
+            if place in ("D", "DY"):
+                for half in ("a", "b"):
+                    self.arrive(place, 1 - c, half, "P" + place + half)
+            else:
+                self.arrive(place, 1 - c, "", "P" + place)
+
+    def cut_weights(ref, half):
+        return ref.at[:, pl.ds(0 if half == "a" else SHARD // 2, SHARD // 2)]
+
+    def cut_pieces(ref, half):
+        return ref.at[pl.ds(0 if half == "a" else 4, 4)]
+
+    wg = [Gather(lambda j, core, n=n: wbuf.at[n, j, core], send.at[n], recv.at[n], cut_weights)
+          for n in range(3)]
+    pg = Gather(lambda j, core: wp.at[j, core], psend, precv, cut_pieces)
+
+    wg[0].own(shard(0))
+    wg[1].own(shard(1))
 
     def layer_norm(vals, shift, scale):
         vals = vals.astype(F32)
@@ -151,21 +205,6 @@
     keep_t = pltpu.make_async_copy(nt.at[s], tnt.at[own_row], own_sem.at[1])
     keep_t.start()
 
-    def pieces(j, carry):
-        to_s, to_h = 2 * j + c, s // 2
-        here = jnp.logical_and(to_s == s, to_h == h)
-
-        @pl.when(jnp.logical_not(here))
-        def _():
-            remote(pv.at[:, j], wp.at[j, c, h], wsend.at[j], wrecv.at[h], to_s, to_h).start()
-
-        @pl.when(here)
-        def _():
-            pltpu.make_async_copy(pv.at[:, j], wp.at[j, c, h], own_sem.at[2]).start()
-        return carry
-
-    lax.fori_loop(0, 8, pieces, 0)
-
     shift = modv[pl.ds(0, 1), :]
     scale = 1.0 + modv[pl.ds(1, 1), :]
 
@@ -175,7 +214,9 @@
             vid[pl.ds(pl.multiple_of(i * 16, 16), 16), :], shift, scale)
         return carry
 
-    lax.fori_loop(0, 40, norm_rows, 0)
+    fetch_vid.wait()
+    lax.fori_loop(0, 40, norm_rows, 0, unroll=4)
+    wg[0].one()
 
     def scattered(d, carry):
         remote(nt.at[0], tnt.at[0], tsend.at[d], trecv.at[d], partner).wait_recv()
@@ -183,25 +224,50 @@
 
     lax.fori_loop(1, 16, scattered, 0)
     keep_t.wait()
+    fetch_wt.wait()
     for g in range(3):
-        cols = pl.ds(g * PART, PART)
-        part[:, :, :, cols] = jnp.dot(
-            tnt[...].reshape(256, SHARD), wt[:, cols], preferred_element_type=F32
+        part[:, :, :, g * PART:(g + 1) * PART] = jnp.dot(
+            tnt[...].reshape(256, SHARD), wt[g], preferred_element_type=F32
         ).reshape(2, 8, 16, PART)
     swap = remote(part.at[1 - c], ppart, rsend.at[0], rrecv.at[0], partner)
     swap.start()
-
-    wg.arrive("L", c, "", "L")
-    wg.push("L", c, "a", "Da", right)
-    wg.arrive("R", c, "", "R")
-    wg.push("R", c, "b", "Db", left)
-    wg.arrive("Y", c, "", "Y")
-    wg.push("Y", c, "", "RY", left)
-    wg.push("Y", c, "", "LY", right)
-    wg.push("L", c, "", "PL", partner)
-    wg.push("R", c, "", "PR", partner)
-    wg.push("Y", c, "", "PY", partner)
-
+    wg[2].own(shard(2))
+    fetch_pv.wait()
+    pv[...] = pvt[...].astype(F32).T.astype(BF).reshape(3, 8, 16, SHARD)
+
+    def pieces(j, carry):
+        to_s, to_h = 2 * j + c, s // 2
+        here = jnp.logical_and(to_s == s, to_h == h)
+
+        @pl.when(jnp.logical_not(here))
+        def _():
+            remote(pv.at[:, j], wp.at[j, c, h], wsend.at[j], wrecv.at[h], to_s, to_h).start()
+
+        @pl.when(here)
+        def _():
+            pltpu.make_async_copy(pv.at[:, j], wp.at[j, c, h], own_sem.at[2]).start()
+        return carry
+
+    lax.fori_loop(0, 8, pieces, 0)
+
+    def multiply(n, place, first=False):
+        wg[n].pair(place)
+        j = slots[place]
+        lhs = normed[:, pl.ds(pl.multiple_of(j * PART, PART), PART)]
+        rhs = jnp.concatenate([wbuf[n, j, :, g].reshape(PART, HD) for g in range(3)], axis=1)
+        term = jnp.dot(lhs, rhs, preferred_element_type=F32)
+        if first:
+            acc[n] = term
+        else:
+            acc[n] += term
+
+    keep[0].wait()
+    multiply(0, "O", True)
+    wg[1].one()
+    multiply(0, "Y")
+    multiply(0, "L")
+    multiply(0, "R")
+    wg[0].two()
     swap.wait()
     part[pl.ds(c, 1)] = part[pl.ds(c, 1)] + ppart[...].reshape(1, 8, 16, WIDE)
 
@@ -212,50 +278,18 @@
 
     lax.fori_loop(1, 8, reduce_send, 0)
 
-    def multiply(place, first=False):
-        j = slots[place]
-        lhs = normed[:, pl.ds(pl.multiple_of(j * PART, PART), PART)]
-        for g in range(3):
-            cols = pl.ds(g * PART, PART)
-            term = jnp.dot(lhs, wbuf[j, :, :, cols].reshape(PART, PART), preferred_element_type=F32)
-            if first:
-                acc[:, cols] = term
-            else:
-                acc[:, cols] += term
-
-    keep.wait()
-    wg.arrive("O", 1 - c, "", "PO")
-    multiply("O", True)
-    wg.arrive("Y", 1 - c, "", "PY")
-    multiply("Y")
-    wg.arrive("L", 1 - c, "", "PL")
-    multiply("L")
-    wg.arrive("D", c, "a", "Da")
-    wg.push("D", c, "a", "DYa", ynbr)
-    wg.push("D", c, "a", "PDa", partner)
-    wg.arrive("D", c, "b", "Db")
-    wg.push("D", c, "b", "DYb", ynbr)
-    wg.push("D", c, "b", "PDb", partner)
-    wg.arrive("R", 1 - c, "", "PR")
-    multiply("R")
-    wg.arrive("LY", c, "", "LY")
-    wg.push("LY", c, "", "PLY", partner)
-    wg.arrive("RY", c, "", "RY")
-    wg.push("RY", c, "", "PRY", partner)
-    wg.arrive("D", 1 - c, "a", "PDa")
-    wg.arrive("D", 1 - c, "b", "PDb")
-    multiply("D")
-    wg.arrive("DY", c, "a", "DYa")
-    wg.push("DY", c, "a", "PDYa", partner)
-    wg.arrive("LY", 1 - c, "", "PLY")
-    multiply("LY")
-    wg.arrive("DY", c, "b", "DYb")
-    wg.push("DY", c, "b", "PDYb", partner)
-    wg.arrive("RY", 1 - c, "", "PRY")
-    multiply("RY")
-    wg.arrive("DY", 1 - c, "a", "PDYa")
-    wg.arrive("DY", 1 - c, "b", "PDYb")
-    multiply("DY")
+    keep[1].wait()
+    multiply(1, "O", True)
+    wg[2].one()
+    multiply(0, "LY")
+    multiply(0, "RY")
+    multiply(0, "D")
+    multiply(1, "Y")
+    multiply(1, "L")
+    multiply(1, "R")
+    wg[1].two()
+    wg[0].three()
+    multiply(0, "DY")
 
     def kv_push(k, n, to, src=None):
         src = kv.at[n] if src is None else src
@@ -267,49 +301,28 @@
         ref = kvbuf.at[k, n]
         remote(ref, ref, ksend.at[k, n], krecv.at[k, n], partner).wait_recv()
 
-    for n in range(3):
-        def finish(i, carry, n=n):
-            rows = pl.ds(pl.multiple_of(i * 128, 128), 128)
-            kv[n, rows, :HD] = head_normed(
-                acc[rows, PART + n * HD:PART + (n + 1) * HD], gainv[pl.ds(1, 1), :]).astype(BF)
-            kv[n, rows, HD:] = acc[rows, 2 * PART + n * HD:2 * PART + (n + 1) * HD].astype(BF)
+    def finish(n):
+        def keys(i, carry):
+            rows = pl.ds(i * 128, 128)
+            kv[n, rows, :HD] = head_normed(acc[n, rows, HD:2 * HD], gainv[pl.ds(1, 1), :]).astype(BF)
+            kv[n, rows, HD:] = acc[n, rows, 2 * HD:].astype(BF)
             return carry
 
-        lax.fori_loop(0, TILES, finish, 0)
+        def queries(i, carry):
+            rows = pl.ds(i * 128, 128)
+            q[n, rows] = head_normed(acc[n, rows, :HD], gainv[pl.ds(0, 1), :]).astype(BF)
+            return carry
+
+        lax.fori_loop(0, TILES, keys, 0, unroll=True)
         kv_push(1, n, ynbr)
-        if n < 2:
-            kv_push(3, n, xnbr)
+        kv_push(3, n, xnbr)
         kv_push(0, n, partner)
-
-    def finish_q(i, carry):
-        rows = pl.ds(pl.multiple_of(i * 128, 128), 128)
-        for n in range(3):
-            q[n, rows] = head_normed(acc[rows, n * HD:(n + 1) * HD], gainv[pl.ds(0, 1), :]).astype(BF)
-        return carry
-
-    lax.fori_loop(0, TILES, finish_q, 0)
-
-    def reduced(d, carry):
-        remote(part.at[0, 0], tsum_in.at[d], rsend.at[d], rrecv.at[d], partner).wait_recv()
-        return carry
-
-    lax.fori_loop(1, 8, reduced, 0)
-    total = part[pl.ds(c, 1), pl.ds(chip, 1)].reshape(16, WIDE)
-    for d in range(1, 8):
-        total = total + tsum_in[d]
-    for n in range(6):
-        hd = total[:, n * HD:(n + 1) * HD]
-        tall[pl.ds(s, 1), :, n * HD:(n + 1) * HD] = head_normed(
-            hd, gaint[pl.ds(n // 3, 1), :]).astype(BF).reshape(1, 16, HD)
-    tall[pl.ds(s, 1), :, 768:] = total[:, 768:].astype(BF).reshape(1, 16, PART)
-
-    def give(d, carry):
-        j = (chip + d) % 8
-        remote(tall.at[s], tall.at[s], gsend.at[d], grecv.at[d], 2 * j + c).start()
-        return carry
-
-    lax.fori_loop(1, 8, give, 0)
-    remote(tall.at[s], tall.at[s], gsend.at[0], grecv.at[0], partner).start()
+        lax.fori_loop(0, TILES, queries, 0, unroll=True)
+
+    def kv_forward(n):
+        kv_arrive(1, n)
+        kv_push(4, n, xnbr, kvbuf.at[1, n])
+        kv_push(2, n, partner, kvbuf.at[1, n])
 
     height = 2 * x + c
     x_there = jnp.where(jnp.logical_or(jnp.logical_and(height == 0, c == 0),
@@ -337,12 +350,12 @@
             top[n, rows, :] = jnp.broadcast_to(new, (128, HD))
             return carry
 
-        lax.fori_loop(0, TILES, tile, 0)
+        lax.fori_loop(0, TILES, tile, 0, unroll=True)
 
     def window_bias(n, dt, dh, there):
         row = h * 3 + n
-        fits = jnp.logical_and(windows[row, 0] >= dt, windows[row, 1] >= dh)
-        reach = jnp.where(fits, windows[row, 2], -1)
+        fits = jnp.logical_and(windows[0, row] >= dt, windows[1, row] >= dh)
+        reach = jnp.where(fits, windows[2, row], -1)
         if there is not None:
             reach = jnp.where(there == 1, reach, -1)
         return lambda i: jnp.where(jnp.abs(lane_tile - i) <= reach, 0.0, NEG_BIG)
@@ -352,24 +365,6 @@
         dh = 1 if k in (0, 2, 3, 4) else 0
         there = x_there if k in (3, 4) else None
         attend(n, lambda: kvbuf[k, n, :, :HD], lambda: kvbuf[k, n, :, HD:], window_bias(n, dt, dh, there))
-
-    for n in range(3):
-        attend(n, lambda n=n: kv[n, :, :HD], lambda n=n: kv[n, :, HD:], window_bias(n, 0, 0, None), True)
-
-    for d in range(1, 8):
-        j = (chip + 8 - d) % 8
-        block = tall.at[2 * j + c]
-        remote(block, block, gsend.at[d], grecv.at[d], partner).wait_recv()
-        remote(block, block, gsend.at[7 + d], grecv.at[7 + d], partner).start()
-    for n in range(3):
-        kv_arrive(0, n)
-        attend_block(0, n)
-    for d in range(1, 8):
-        j = (chip + 8 - d) % 8
-        block = tall.at[2 * j + 1 - c]
-        remote(block, block, gsend.at[7 + d], grecv.at[7 + d], partner).wait_recv()
-    block = tall.at[partner]
-    remote(block, block, gsend.at[0], grecv.at[0], partner).wait_recv()
 
     def text_cols(g, n):
         return tall[:, :, g * PART + n * HD:g * PART + (n + 1) * HD].reshape(256, HD)
@@ -392,15 +387,6 @@
         ts[blocks, :, PART:] = stat.reshape(8, 16, HD)
         return carry
 
-    lax.fori_loop(0, 2, text_part, 0)
-
-    def merge_send(d, carry):
-        to = (s + d) % 16
-        remote(ts.at[to], ts_in.at[d], msend.at[d], mrecv.at[d], to).start()
-        return carry
-
-    lax.fori_loop(1, 16, merge_send, 0)
-
     text_row = jnp.where(lax.broadcasted_iota(jnp.int32, (1, 256), 1) < text_len[0], 0.0, NEG_BIG)
 
     def attend_text(n):
@@ -427,65 +413,129 @@
                 att[n, rows, :HD] / att[n, rows, HD:]).astype(BF).reshape(1, 128, HD)
             return carry
 
-        lax.fori_loop(0, TILES, tile, 0)
+        lax.fori_loop(0, TILES, tile, 0, unroll=True)
         ring_push("O", n, "", "H", hn)
         ring_push("O", n, "", "Dn", up)
         ring_push("O", n, "", "Up", dn)
 
     def ring_one(n):
-        ring_arrive("H", n, "", "H")
-        ring_push("H", n, "", "HDn", up)
-        ring_push("H", n, "", "HUp", dn)
         ring_arrive("Dn", n, "", "Dn")
         ring_push("Dn", n, "a", "D2a", up)
         ring_arrive("Up", n, "", "Up")
         ring_push("Up", n, "b", "D2b", dn)
+        ring_arrive("H", n, "", "H")
+        ring_push("H", n, "", "HDn", up)
+        ring_push("H", n, "", "HUp", dn)
 
     def ring_two(n):
-        ring_arrive("HDn", n, "", "HDn")
-        ring_push("HDn", n, "a", "HD2a", up)
-        ring_arrive("HUp", n, "", "HUp")
-        ring_push("HUp", n, "b", "HD2b", dn)
-
-    def ring_three(n):
         for half in ("a", "b"):
             ring_arrive("D2", n, half, "D2" + half)
+            ring_push("D2", n, half, "HD2" + half, hn)
+
+    def ring_three(n):
+        ring_arrive("HDn", n, "", "HDn")
+        ring_arrive("HUp", n, "", "HUp")
+        for half in ("a", "b"):
             ring_arrive("HD2", n, half, "HD2" + half)
 
     def project(n, first=False):
-        def one(j, carry):
+        for j in range(0, 8, 2):
             rhs = jnp.concatenate(
-                [wp[:, 0, j, n].reshape(HD, SHARD), wp[:, 1, j, n].reshape(HD, SHARD)], axis=1)
-            acc2[...] += jnp.dot(attbuf[j, n], rhs, preferred_element_type=F32)
-            return carry
-
-        lax.fori_loop(0, 8, one, 0)
-
-    kv_arrive(1, 0)
-    kv_push(4, 0, xnbr, kvbuf.at[1, 0])
-    kv_push(3, 2, xnbr)
-    kv_push(2, 0, partner, kvbuf.at[1, 0])
+                [jnp.concatenate([wp[:, core, j + e, n].reshape(HD, SHARD) for core in range(2)], axis=1)
+                 for e in range(2)], axis=0)
+            lhs = jnp.concatenate([attbuf[j, n], attbuf[j + 1, n]], axis=1)
+            term = jnp.dot(lhs, rhs, preferred_element_type=F32)
+            if first and j == 0:
+                acc2[...] = term
+            else:
+                acc2[...] += term
+
+    def attend_own(n):
+        attend(n, lambda: kv[n, :, :HD], lambda: kv[n, :, HD:], window_bias(n, 0, 0, None), True)
+
+    def attend_other(k, n):
+        if k != 1:
+            kv_arrive(k, n)
+        attend_block(k, n)
+
+    finish(0)
+    attend_own(0)
+    multiply(1, "LY")
+    multiply(1, "RY")
+    multiply(1, "D")
+    keep[2].wait()
+    multiply(2, "O", True)
+    multiply(2, "Y")
+    multiply(2, "L")
+    multiply(2, "R")
+    wg[2].two()
+    wg[1].three()
+    multiply(1, "DY")
+    finish(1)
+    kv_forward(0)
+
+    def reduced(d, carry):
+        remote(part.at[0, 0], tsum_in.at[d], rsend.at[d], rrecv.at[d], partner).wait_recv()
+        return carry
+
+    lax.fori_loop(1, 8, reduced, 0)
+    total = part[pl.ds(c, 1), pl.ds(chip, 1)].reshape(16, WIDE)
+    for d in range(1, 8):
+        total = total + tsum_in[d]
+    for n in range(6):
+        hd = total[:, n * HD:(n + 1) * HD]
+        tall[pl.ds(s, 1), :, n * HD:(n + 1) * HD] = head_normed(
+            hd, gaint[pl.ds(n // 3, 1), :]).astype(BF).reshape(1, 16, HD)
+    tall[pl.ds(s, 1), :, 768:] = total[:, 768:].astype(BF).reshape(1, 16, PART)
+
+    def give(d, carry):
+        j = (chip + d) % 8
+        remote(tall.at[s], tall.at[s], gsend.at[d], grecv.at[d], 2 * j + c).start()
+        return carry
+
+    lax.fori_loop(1, 8, give, 0)
+    remote(tall.at[s], tall.at[s], gsend.at[0], grecv.at[0], partner).start()
+
+    attend_own(1)
+    attend_other(0, 0)
+    attend_other(1, 0)
+    multiply(2, "LY")
+    multiply(2, "RY")
+    multiply(2, "D")
+    wg[2].three()
+    multiply(2, "DY")
+    finish(2)
+
+    for d in range(1, 8):
+        j = (chip + 8 - d) % 8
+        block = tall.at[2 * j + c]
+        remote(block, block, gsend.at[d], grecv.at[d], partner).wait_recv()
+        remote(block, block, gsend.at[7 + d], grecv.at[7 + d], partner).start()
+    attend_own(2)
+    attend_other(0, 1)
+    attend_other(2, 0)
+    attend_other(3, 0)
+    kv_forward(1)
+    attend_other(1, 1)
+    for d in range(1, 8):
+        j = (chip + 8 - d) % 8
+        block = tall.at[2 * j + 1 - c]
+        remote(block, block, gsend.at[7 + d], grecv.at[7 + d], partner).wait_recv()
+    block = tall.at[partner]
+    remote(block, block, gsend.at[0], grecv.at[0], partner).wait_recv()
+    lax.fori_loop(0, 2, text_part, 0, unroll=True)
+
+    def merge_send(d, carry):
+        to = (s + d) % 16
+        remote(ts.at[to], ts_in.at[d], msend.at[d], mrecv.at[d], to).start()
+        return carry
+
+    lax.fori_loop(1, 16, merge_send, 0)
     attend_text(0)
-    attend_block(1, 0)
-    kv_arrive(2, 0)
-    attend_block(2, 0)
-    kv_arrive(3, 0)
-    attend_block(3, 0)
+    attend_other(4, 0)
+    close_head(0)
     attend_text(1)
     attend_text(2)
-    kv_arrive(4, 0)
-    attend_block(4, 0)
-    close_head(0)
-
-    kv_arrive(1, 1)
-    kv_push(4, 1, xnbr, kvbuf.at[1, 1])
-    kv_push(2, 1, partner, kvbuf.at[1, 1])
-    attend_block(1, 1)
-    kv_arrive(2, 1)
-    attend_block(2, 1)
-    kv_arrive(3, 1)
-    attend_block(3, 1)
-    ring_one(0)
 
     def piece(j, carry):
         @pl.when(jnp.logical_not(jnp.logical_and(s // 2 == h, j == h)))
@@ -499,25 +549,18 @@
     def _():
         pltpu.make_async_copy(pv.at[:, 0], wp.at[chip, c, h], own_sem.at[2]).wait()
 
-    pg.push("O", c, "", "Y", ynbr)
-    pg.push("O", c, "", "L", right)
-    pg.push("O", c, "", "R", left)
-    pg.push("O", c, "", "PO", partner)
-
-    kv_arrive(4, 1)
-    attend_block(4, 1)
+    attend_other(0, 2)
+    attend_other(2, 1)
+    attend_other(3, 1)
+    kv_forward(2)
+    pg.own()
+    attend_other(1, 2)
+    attend_other(4, 1)
     close_head(1)
-    ring_two(0)
-
-    kv_arrive(1, 2)
-    kv_push(4, 2, xnbr, kvbuf.at[1, 2])
-    kv_push(2, 2, partner, kvbuf.at[1, 2])
-    attend_block(1, 2)
-    kv_arrive(2, 2)
-    attend_block(2, 2)
-    kv_arrive(3, 2)
-    attend_block(3, 2)
-    ring_one(1)
+    ring_one(0)
+    attend_other(2, 2)
+    attend_other(3, 2)
+    pg.one()
 
     def merge_wait(d, carry):
         remote(ts.at[0], ts_in.at[d], msend.at[d], mrecv.at[d], partner).wait_recv()
@@ -551,41 +594,22 @@
 
     lax.fori_loop(1, 16, text_give, 0)
 
-    pg.arrive("L", c, "", "L")
-    pg.push("L", c, "a", "Da", right)
-    pg.arrive("R", c, "", "R")
-    pg.push("R", c, "b", "Db", left)
-    pg.arrive("Y", c, "", "Y")
-    pg.push("Y", c, "", "RY", left)
-    pg.push("Y", c, "", "LY", right)
-    pg.push("L", c, "", "PL", partner)
-    pg.push("R", c, "", "PR", partner)
-    pg.push("Y", c, "", "PY", partner)
-
-    kv_arrive(4, 2)
-    attend_block(4, 2)
+    attend_other(4, 2)
     close_head(2)
-    ring_two(1)
-
-    pg.arrive("D", c, "a", "Da")
-    pg.push("D", c, "a", "DYa", ynbr)
-    pg.push("D", c, "a", "PDa", partner)
-    pg.arrive("D", c, "b", "Db")
-    pg.push("D", c, "b", "DYb", ynbr)
-    pg.push("D", c, "b", "PDb", partner)
-    pg.arrive("LY", c, "", "LY")
-    pg.push("LY", c, "", "PLY", partner)
-    pg.arrive("RY", c, "", "RY")
-    pg.push("RY", c, "", "PRY", partner)
-
+    ring_two(0)
+    ring_one(1)
+    pg.two()
+
+    fetch_pt.wait()
     def text_given(d, carry):
         block = atg.at[(s + 16 - d) % 16]
         remote(block, block, asend.at[d], arecv.at[d], partner).wait_recv()
         return carry
 
     lax.fori_loop(1, 16, text_given, 0)
-    tpart[...] = jnp.dot(atg[...].reshape(256, PART), pt[...],
-                         preferred_element_type=F32).reshape(16, 16, SHARD)
+    tpart[...] = lax.dot_general(
+        atg[...].reshape(256, PART), pt[...], (((1,), (1,)), ((), ())),
+        preferred_element_type=F32).reshape(16, 16, SHARD)
 
     def text_move(i, carry):
         here = jnp.logical_and(i == s, s // 2 == h)
@@ -602,19 +626,12 @@
     lax.fori_loop(0, 16, text_move, 0)
 
     ring_one(2)
-    pg.arrive("DY", c, "a", "DYa")
-    pg.push("DY", c, "a", "PDYa", partner)
-    pg.arrive("DY", c, "b", "DYb")
-    pg.push("DY", c, "b", "PDYb", partner)
-    pg.arrive("O", 1 - c, "", "PO")
-    for place in ("Y", "L", "R", "LY", "RY"):
-        pg.arrive(place, 1 - c, "", "P" + place)
-    for half in ("a", "b"):
-        pg.arrive("D", 1 - c, half, "PD" + half)
-        pg.arrive("DY", 1 - c, half, "PDY" + half)
-    acc2[...] = jnp.zeros_like(acc2)
+    ring_two(1)
+    pg.three()
+    for place in ("O", "Y", "L", "R", "LY", "RY", "D", "DY"):
+        pg.pair(place)
     ring_three(0)
-    project(0)
+    project(0, True)
     ring_two(2)
     ring_three(1)
     project(1)
@@ -646,7 +663,7 @@
         video_out[rows, :] = (vid[rows, out_cols].astype(F32) + gate * acc2[at, :]).astype(BF)
         return carry
 
-    lax.fori_loop(0, 40, write, 0)
+    lax.fori_loop(0, 40, write, 0, unroll=4)
 
     def left_t(d, carry):
         remote(nt.at[0], tnt.at[0], tsend.at[d], trecv.at[d], partner).wait_send()
@@ -690,16 +707,19 @@
 def block_kernel(vid, txt, modv, modt, w, wt, pv, pt, gainv, gaint, windows, text_len):
     vm = pl.BlockSpec(memory_space=pltpu.VMEM)
     sm = pl.BlockSpec(memory_space=pltpu.SMEM)
+    hbm = pl.BlockSpec(memory_space=pl.ANY)
     dma = pltpu.SemaphoreType.DMA
     v = pltpu.VMEM
     return pl.pallas_call(
         kernel,
         name="attention_block",
         out_shape=(jax.ShapeDtypeStruct((ROWS, PART), BF), jax.ShapeDtypeStruct((16, PART), BF)),
-        in_specs=[vm] * 10 + [sm, sm],
+        in_specs=[hbm] + [vm] * 3 + [hbm] * 4 + [vm] * 2 + [sm, sm],
         out_specs=(vm, vm),
         scratch_shapes=[
-            v((ROWS, 3072), BF), v((8, 2, SHARD, WIDE), BF), v((ROWS, WIDE), F32),
+            v((ROWS, 3072), BF), v((3, SHARD, PART), BF), v((SHARD, PART), BF), v((SHARD, PART), BF),
+            v((3, 8, 16, SHARD), BF),
+            v((ROWS, 3072), BF), v((3, 8, 2, 3, SHARD, HD), BF), v((3, ROWS, PART), F32),
             v((16, 16, SHARD), BF), v((16, 16, SHARD), BF),
             v((2, 8, 16, WIDE), F32), v((8, 16, WIDE), F32), v((8, 16, WIDE), F32),
             v((16, 16, WIDE), BF),
@@ -708,7 +728,7 @@
             v((8, 2, 8, 3, 16, SHARD), BF), v((ROWS, PART), F32),
             v((16, 16, 512), F32), v((16, 16, 512), F32), v((16, 16, PART), BF),
             v((16, 16, SHARD), F32), v((2, 8, 16, SHARD), F32),
-            dma((4,)), dma((19,)), dma((19,)), dma((16,)), dma((16,)),
+            dma((11,)), dma((3, 19)), dma((3, 19)), dma((16,)), dma((16,)),
             dma((8,)), dma((8,)), dma((15,)), dma((15,)),
             dma((5, 3)), dma((5, 3)), dma((9, 3)), dma((9, 3)),
             dma((8,)), dma((8,)), dma((19,)), dma((19,)),
@@ -723,9 +743,9 @@
          gain_video, gain_text, windows, text_len):
     return block_kernel(
         video_in, text_in, mod_video, mod_text,
-        qkv_video.reshape(SHARD, WIDE), qkv_text.reshape(SHARD, WIDE),
-        proj_video.reshape(3, 8, 16, SHARD), proj_text,
-        gain_video, gain_text, windows, text_len)
+        jnp.transpose(qkv_video, (1, 0, 2)), jnp.transpose(qkv_text, (1, 0, 2)),
+        proj_video.T, proj_text.T,
+        gain_video, gain_text, windows.T, text_len)
 
 
 def solution(mesh):

time: 179 us -> 126 us (0.70)
  Pallas kernels: 166 us -> 121 us
  local copies, waits for them, and re-layouts: 11.6 us -> 3.16 us
    pallas_call x1, Pallas kernels: 166 us -> 121 us  [block_kernel(): pl.pallas_call(kernel, name='attention_block', out_shape=(jax.ShapeDtypeS...]
    unnamed x5 -> x2, local copies, waits for them, and re-layouts: 7.98 us -> 3.16 us
    reshape x2 -> x0, local copies, waits for them, and re-layouts: 3.64 us -> none  [the longest x1 1.83 us: body(): qkv_text.reshape(SHARD, WIDE)]
where the time goes in v2:
time: 126 us; the launch traced here: 125 us
  Pallas kernels  121 us (96%)
  local copies, waits for them, and re-layouts  3.16 us (3%)
  between operations  1.29 us (1%)
    pallas_call x1, Pallas kernels, block_kernel(): pl.pallas_call(kernel, name='attention_block', out_shape=(jax.ShapeDtypeS...  121 us
    unnamed x2, local copies, waits for them, and re-layouts  3.16 us

profile of v2, /device:TPU:1, one launch (start us, length us, event | category | flops | bytes accessed | tf_op | source)
XLA Modules:
  0.0 125.5 jit_solution(15790670223073013550)
XLA Ops:
  1.3 121.0 %attention_block.1 = (bf16[640,384]{1,0:T(8,128)(2,1)}, bf16[16,384]{1,0:T(8,128)(2,1)}) custom-call(bf16[640,3072]{1,0:T(8,128)(2,1)} %vid_hbm.1, bf16[16,3072]{1,0:T(8,128)(2,1)} %txt.1, f32[3,3072]{1,0:T(4,128)} %modv.1, f32[3,3072]{1,0:T(4,128)} %modt.1, bf16[3,192,384]{2,1,0:T(8,128)(2,1)} %bitcast.5, bf16[3,192,384]{2,1,0:T(8,128)(2,1)} %bitcast.6, ...), custom_call_target="tpu_custom_call" | custom-call | tf_op jit(solution)/shard_map/attention_block/pallas_call | solution.py:713
  122.3 1.9 %copy.17 = bf16[640,384]{1,0:T(8,128)(2,1)} copy(bf16[640,384]{1,0:T(8,128)(2,1)} %get-tuple-element.4) | data formatting | bytes 983040
  124.2 1.3 %copy.18 = bf16[16,384]{1,0:T(8,128)(2,1)} copy(bf16[16,384]{1,0:T(8,128)(2,1)} %get-tuple-element.5) | data formatting | bytes 24576

commit v3 on v2

--- a/solution.py
+++ b/solution.py
@@ -110,6 +110,15 @@
         return carry
 
     lax.fori_loop(0, 16, greet_far, 0)
+    def layer_norm(vals, shift, scale):
+        vals = vals.astype(F32)
+        vals = vals - jnp.mean(vals, axis=1, keepdims=True)
+        spread = jnp.mean(jnp.square(vals), axis=1, keepdims=True)
+        return (vals * lax.rsqrt(spread + 1e-6) * scale + shift).astype(BF)
+
+    text_normed = layer_norm(txt[...], modt[pl.ds(0, 1), :], 1.0 + modt[pl.ds(1, 1), :])
+    for d in range(16):
+        nt[d] = text_normed[:, d * SHARD:(d + 1) * SHARD]
     pl.semaphore_wait(barrier, 15 + 3 + 16 - home)
 
     sent = []
@@ -183,17 +192,7 @@
     pg = Gather(lambda j, core: wp.at[j, core], psend, precv, cut_pieces)
 
     wg[0].own(shard(0))
-    wg[1].own(shard(1))
-
-    def layer_norm(vals, shift, scale):
-        vals = vals.astype(F32)
-        vals = vals - jnp.mean(vals, axis=1, keepdims=True)
-        spread = jnp.mean(jnp.square(vals), axis=1, keepdims=True)
-        return (vals * lax.rsqrt(spread + 1e-6) * scale + shift).astype(BF)
-
-    text_normed = layer_norm(txt[...], modt[pl.ds(0, 1), :], 1.0 + modt[pl.ds(1, 1), :])
-    for d in range(16):
-        nt[d] = text_normed[:, d * SHARD:(d + 1) * SHARD]
+
     own_row = c * 8 + chip
 
     def scatter(d, carry):
@@ -204,6 +203,7 @@
     lax.fori_loop(1, 16, scatter, 0)
     keep_t = pltpu.make_async_copy(nt.at[s], tnt.at[own_row], own_sem.at[1])
     keep_t.start()
+    wg[1].own(shard(1))
 
     shift = modv[pl.ds(0, 1), :]
     scale = 1.0 + modv[pl.ds(1, 1), :]
@@ -263,21 +263,17 @@
 
     keep[0].wait()
     multiply(0, "O", True)
+    swap.wait()
+    part[pl.ds(c, 1)] = part[pl.ds(c, 1)] + ppart[...].reshape(1, 8, 16, WIDE)
+
+    across = remote(part.at[c, pl.ds((1 - y) * 4, 4)], tsum_in.at[pl.ds(0, 4)],
+                    rsend.at[1], rrecv.at[1], ynbr)
+    across.start()
     wg[1].one()
     multiply(0, "Y")
     multiply(0, "L")
     multiply(0, "R")
     wg[0].two()
-    swap.wait()
-    part[pl.ds(c, 1)] = part[pl.ds(c, 1)] + ppart[...].reshape(1, 8, 16, WIDE)
-
-    def reduce_send(d, carry):
-        j = (chip + d) % 8
-        remote(part.at[c, j], tsum_in.at[d], rsend.at[d], rrecv.at[d], 2 * j + c).start()
-        return carry
-
-    lax.fori_loop(1, 8, reduce_send, 0)
-
     keep[1].wait()
     multiply(1, "O", True)
     wg[2].one()
@@ -290,7 +286,6 @@
     wg[1].two()
     wg[0].three()
     multiply(0, "DY")
-
     def kv_push(k, n, to, src=None):
         src = kv.at[n] if src is None else src
         cp = remote(src, kvbuf.at[k, n], ksend.at[k, n], krecv.at[k, n], to)
@@ -329,7 +324,7 @@
                                        jnp.logical_and(height == 7, c == 1)), 0, 1)
     lane_tile = lax.broadcasted_iota(jnp.int32, (1, ROWS), 1) // 128
 
-    def attend(n, keys, values, bias_of, first=False):
+    def attend(n, keys, values, bias_of, first=False, tiles=(0, TILES)):
         def tile(i, carry):
             rows = pl.ds(pl.multiple_of(i * 128, 128), 128)
             t = lax.dot_general(q[n, rows], keys(), (((1,), (1,)), ((), ())),
@@ -350,7 +345,7 @@
             top[n, rows, :] = jnp.broadcast_to(new, (128, HD))
             return carry
 
-        lax.fori_loop(0, TILES, tile, 0, unroll=True)
+        lax.fori_loop(*tiles, tile, 0, unroll=True)
 
     def window_bias(n, dt, dh, there):
         row = h * 3 + n
@@ -360,11 +355,11 @@
             reach = jnp.where(there == 1, reach, -1)
         return lambda i: jnp.where(jnp.abs(lane_tile - i) <= reach, 0.0, NEG_BIG)
 
-    def attend_block(k, n):
+    def attend_block(k, n, tiles=(0, TILES)):
         dt = 1 if k in (1, 2, 4) else 0
         dh = 1 if k in (0, 2, 3, 4) else 0
         there = x_there if k in (3, 4) else None
-        attend(n, lambda: kvbuf[k, n, :, :HD], lambda: kvbuf[k, n, :, HD:], window_bias(n, dt, dh, there))
+        attend(n, lambda: kvbuf[k, n, :, :HD], lambda: kvbuf[k, n, :, HD:], window_bias(n, dt, dh, there), False, tiles)
 
     def text_cols(g, n):
         return tall[:, :, g * PART + n * HD:g * PART + (n + 1) * HD].reshape(256, HD)
@@ -382,9 +377,13 @@
             peak = jnp.max(t, axis=1, keepdims=True)
             p = jnp.exp2(t - peak).astype(BF)
             both = jnp.dot(p, with_ones(kv[n, :, HD:]), preferred_element_type=F32)
-            ts[blocks, :, n * HD:(n + 1) * HD] = (both[:, :HD] / both[:, HD:]).reshape(8, 16, HD)
-            stat = jnp.where(lanes == n, peak + jnp.log2(both[:, HD:]), stat)
-        ts[blocks, :, PART:] = stat.reshape(8, 16, HD)
+            ts[blocks, :, n * HD:(n + 1) * HD] = (both[:, :HD] / both[:, HD:]).astype(BF).reshape(8, 16, HD)
+            level = peak + jnp.log2(both[:, HD:])
+            for e in range(3):
+                piece_of = level.astype(BF).astype(F32)
+                stat = jnp.where(lanes == 3 * e + n, piece_of, stat)
+                level = level - piece_of
+        ts[blocks, :, PART:] = stat.astype(BF).reshape(8, 16, HD)
         return carry
 
     text_row = jnp.where(lax.broadcasted_iota(jnp.int32, (1, 256), 1) < text_len[0], 0.0, NEG_BIG)
@@ -392,31 +391,38 @@
     def attend_text(n):
         attend(n, lambda: text_cols(1, n), lambda: text_cols(2, n), lambda i: text_row)
 
+    chunks = ((0, 0, ROWS), (1, 0, ROWS), (2, 0, 384), (2, 384, 256))
+
+    def ring_view(place, k, half):
+        n, base, size = chunks[k]
+        if half:
+            size = size // 2
+            base = base + (size if half == "b" else 0)
+        return attbuf.at[places[place], n, pl.ds(base, size)]
+
     def ring_push(place, n, half, kind, to):
-        ref = attbuf.at[places[place], n]
-        if half:
-            ref = ref.at[pl.ds(0 if half == "a" else ROWS // 2, ROWS // 2)]
+        ref = ring_view(place, n, half)
         cp = remote(ref, ref, zsend.at[RID[kind], n], zrecv.at[RID[kind], n], None, to)
         cp.start()
         sent.append(cp)
 
     def ring_arrive(place, n, half, kind):
-        ref = attbuf.at[places[place], n]
-        if half:
-            ref = ref.at[pl.ds(0 if half == "a" else ROWS // 2, ROWS // 2)]
+        ref = ring_view(place, n, half)
         remote(ref, ref, zsend.at[RID[kind], n], zrecv.at[RID[kind], n], None, up).wait_recv()
 
-    def close_head(n):
+    def close_head(k):
+        n, base, size = chunks[k]
+
         def tile(i, carry):
-            rows = pl.ds(pl.multiple_of(i * 128, 128), 128)
+            rows = pl.ds(i * 128, 128)
             attbuf[pl.ds(h, 1), n, rows, :] = (
                 att[n, rows, :HD] / att[n, rows, HD:]).astype(BF).reshape(1, 128, HD)
             return carry
 
-        lax.fori_loop(0, TILES, tile, 0, unroll=True)
-        ring_push("O", n, "", "H", hn)
-        ring_push("O", n, "", "Dn", up)
-        ring_push("O", n, "", "Up", dn)
+        lax.fori_loop(base // 128, (base + size) // 128, tile, 0, unroll=True)
+        ring_push("O", k, "", "H", hn)
+        ring_push("O", k, "", "Dn", up)
+        ring_push("O", k, "", "Up", dn)
 
     def ring_one(n):
         ring_arrive("Dn", n, "", "Dn")
@@ -438,17 +444,19 @@
         for half in ("a", "b"):
             ring_arrive("HD2", n, half, "HD2" + half)
 
-    def project(n, first=False):
+    def project(k):
+        n, base, size = chunks[k]
+        rows = pl.ds(base, size)
         for j in range(0, 8, 2):
             rhs = jnp.concatenate(
                 [jnp.concatenate([wp[:, core, j + e, n].reshape(HD, SHARD) for core in range(2)], axis=1)
                  for e in range(2)], axis=0)
-            lhs = jnp.concatenate([attbuf[j, n], attbuf[j + 1, n]], axis=1)
+            lhs = jnp.concatenate([attbuf[j, n, rows], attbuf[j + 1, n, rows]], axis=1)
             term = jnp.dot(lhs, rhs, preferred_element_type=F32)
-            if first and j == 0:
-                acc2[...] = term
+            if n == 0 and j == 0:
+                acc2[rows, :] = term
             else:
-                acc2[...] += term
+                acc2[rows, :] += term
 
     def attend_own(n):
         attend(n, lambda: kv[n, :, :HD], lambda: kv[n, :, HD:], window_bias(n, 0, 0, None), True)
@@ -459,6 +467,15 @@
         attend_block(k, n)
 
     finish(0)
+    across.wait()
+    part[pl.ds(c, 1), pl.ds(y * 4, 4)] = (
+        part[pl.ds(c, 1), pl.ds(y * 4, 4)] + tsum_in[0:4].reshape(1, 4, 16, WIDE))
+    along = []
+    for d in range(1, 4):
+        xo = (x + d) % 4
+        along.append(remote(part.at[c, y * 4 + xo], tsum_in.at[4 + d], rsend.at[1 + d],
+                            rrecv.at[1 + d], seq_of(y, xo, c)))
+        along[-1].start()
     attend_own(0)
     multiply(1, "LY")
     multiply(1, "RY")
@@ -469,18 +486,10 @@
     multiply(2, "L")
     multiply(2, "R")
     wg[2].two()
-    wg[1].three()
-    multiply(1, "DY")
-    finish(1)
-    kv_forward(0)
-
-    def reduced(d, carry):
-        remote(part.at[0, 0], tsum_in.at[d], rsend.at[d], rrecv.at[d], partner).wait_recv()
-        return carry
-
-    lax.fori_loop(1, 8, reduced, 0)
+    for cp in along:
+        cp.wait()
     total = part[pl.ds(c, 1), pl.ds(chip, 1)].reshape(16, WIDE)
-    for d in range(1, 8):
+    for d in range(5, 8):
         total = total + tsum_in[d]
     for n in range(6):
         hd = total[:, n * HD:(n + 1) * HD]
@@ -488,13 +497,25 @@
             hd, gaint[pl.ds(n // 3, 1), :]).astype(BF).reshape(1, 16, HD)
     tall[pl.ds(s, 1), :, 768:] = total[:, 768:].astype(BF).reshape(1, 16, PART)
 
-    def give(d, carry):
-        j = (chip + d) % 8
-        remote(tall.at[s], tall.at[s], gsend.at[d], grecv.at[d], 2 * j + c).start()
-        return carry
-
-    lax.fori_loop(1, 8, give, 0)
-    remote(tall.at[s], tall.at[s], gsend.at[0], grecv.at[0], partner).start()
+    def text_block(yy, d, core):
+        return tall.at[seq_of(yy, (x + 4 - d) % 4, core)]
+
+    def text_push(k, block, to):
+        cp = remote(block, block, gsend.at[k], grecv.at[k], to)
+        cp.start()
+        sent.append(cp)
+
+    def text_arrive(k, block):
+        remote(block, block, gsend.at[k], grecv.at[k], partner).wait_recv()
+
+    for d in range(1, 4):
+        text_push(d, text_block(y, 0, c), seq_of(y, (x + d) % 4, c))
+    text_push(4, text_block(y, 0, c), ynbr)
+    text_push(0, text_block(y, 0, c), partner)
+    wg[1].three()
+    multiply(1, "DY")
+    finish(1)
+    kv_forward(0)
 
     attend_own(1)
     attend_other(0, 0)
@@ -505,24 +526,24 @@
     wg[2].three()
     multiply(2, "DY")
     finish(2)
-
-    for d in range(1, 8):
-        j = (chip + 8 - d) % 8
-        block = tall.at[2 * j + c]
-        remote(block, block, gsend.at[d], grecv.at[d], partner).wait_recv()
-        remote(block, block, gsend.at[7 + d], grecv.at[7 + d], partner).start()
+    for d in range(1, 4):
+        text_arrive(d, text_block(y, d, c))
+        text_push(4 + d, text_block(y, d, c), ynbr)
+        text_push(7 + d, text_block(y, d, c), partner)
     attend_own(2)
     attend_other(0, 1)
     attend_other(2, 0)
     attend_other(3, 0)
     kv_forward(1)
+    for d in range(4):
+        text_arrive(4 + d, text_block(1 - y, d, c))
+        text_push(11 + d, text_block(1 - y, d, c), partner)
     attend_other(1, 1)
-    for d in range(1, 8):
-        j = (chip + 8 - d) % 8
-        block = tall.at[2 * j + 1 - c]
-        remote(block, block, gsend.at[7 + d], grecv.at[7 + d], partner).wait_recv()
-    block = tall.at[partner]
-    remote(block, block, gsend.at[0], grecv.at[0], partner).wait_recv()
+    for d in range(4):
+        text_arrive(0 if d == 0 else 7 + d, text_block(y, d, 1 - c))
+        text_arrive(11 + d, text_block(1 - y, d, 1 - c))
+
+    attend_text(0)
     lax.fori_loop(0, 2, text_part, 0, unroll=True)
 
     def merge_send(d, carry):
@@ -531,12 +552,9 @@
         return carry
 
     lax.fori_loop(1, 16, merge_send, 0)
-    attend_text(0)
     attend_other(4, 0)
     close_head(0)
     attend_text(1)
-    attend_text(2)
-
     def piece(j, carry):
         @pl.when(jnp.logical_not(jnp.logical_and(s // 2 == h, j == h)))
         def _():
@@ -549,25 +567,34 @@
     def _():
         pltpu.make_async_copy(pv.at[:, 0], wp.at[chip, c, h], own_sem.at[2]).wait()
 
-    attend_other(0, 2)
+    pg.own()
     attend_other(2, 1)
     attend_other(3, 1)
     kv_forward(2)
-    pg.own()
+    attend_other(0, 2)
     attend_other(1, 2)
+    attend_text(2)
+    ring_one(0)
     attend_other(4, 1)
     close_head(1)
-    ring_one(0)
+    pg.one()
     attend_other(2, 2)
     attend_other(3, 2)
-    pg.one()
-
+    ring_two(0)
+    kv_arrive(4, 2)
+    attend_block(4, 2, (0, 3))
+    close_head(2)
+    attend_block(4, 2, (3, TILES))
+    close_head(3)
+    ring_one(1)
+    pg.two()
     def merge_wait(d, carry):
         remote(ts.at[0], ts_in.at[d], msend.at[d], mrecv.at[d], partner).wait_recv()
         return carry
 
     lax.fori_loop(1, 16, merge_wait, 0)
     ts_in[0] = ts[pl.ds(s, 1)].reshape(16, 512)
+    levels = [ts_in[d, :, PART:].astype(F32) for d in range(16)]
     for n in range(3):
         tq = tall[pl.ds(s, 1), :, n * HD:(n + 1) * HD].reshape(16, HD)
         t = lax.dot_general(tq, text_cols(1, n), (((1,), (1,)), ((), ())),
@@ -575,7 +602,7 @@
         peak = jnp.max(t, axis=1, keepdims=True)
         p = jnp.exp2(t - peak).astype(BF)
         both = jnp.dot(p, with_ones(text_cols(2, n)), preferred_element_type=F32)
-        logs = [ts_in[d, :, PART + n:PART + n + 1] for d in range(16)]
+        logs = [v[:, n:n + 1] + v[:, n + 3:n + 4] + v[:, n + 6:n + 7] for v in levels]
         high = peak + jnp.log2(both[:, HD:HD + 1])
         for value in logs:
             high = jnp.maximum(high, value)
@@ -584,7 +611,7 @@
         lower = both[:, HD:HD + 1] * weight
         for d in range(16):
             weight = jnp.exp2(logs[d] - high)
-            upper = upper + ts_in[d, :, n * HD:(n + 1) * HD] * weight
+            upper = upper + ts_in[d, :, n * HD:(n + 1) * HD].astype(F32) * weight
             lower = lower + weight
         atg[pl.ds(s, 1), :, n * HD:(n + 1) * HD] = (upper / lower).astype(BF).reshape(1, 16, HD)
 
@@ -594,12 +621,11 @@
 
     lax.fori_loop(1, 16, text_give, 0)
 
-    attend_other(4, 2)
-    close_head(2)
-    ring_two(0)
-    ring_one(1)
-    pg.two()
-
+    ring_one(2)
+    ring_two(1)
+    ring_one(3)
+    ring_two(2)
+    pg.three()
     fetch_pt.wait()
     def text_given(d, carry):
         block = atg.at[(s + 16 - d) % 16]
@@ -625,16 +651,15 @@
 
     lax.fori_loop(0, 16, text_move, 0)
 
-    ring_one(2)
-    ring_two(1)
-    pg.three()
+    ring_two(3)
     for place in ("O", "Y", "L", "R", "LY", "RY", "D", "DY"):
         pg.pair(place)
     ring_three(0)
-    project(0, True)
-    ring_two(2)
+    project(0)
     ring_three(1)
     project(1)
+    ring_three(2)
+    project(2)
 
     def text_moved(i, carry):
         @pl.when(jnp.logical_not(jnp.logical_and(2 * h + i % 2 == s, i // 2 == h)))
@@ -653,8 +678,8 @@
     sums = jnp.concatenate([jnp.sum(tpart_in[0], axis=0), jnp.sum(tpart_in[1], axis=0)], axis=1)
     text_out[...] = (txt[:, out_cols].astype(F32) + modt[pl.ds(2, 1), out_cols] * sums).astype(BF)
 
-    ring_three(2)
-    project(2)
+    ring_three(3)
+    project(3)
     gate = modv[pl.ds(2, 1), out_cols]
 
     def write(i, carry):
@@ -672,18 +697,6 @@
         return carry
 
     lax.fori_loop(1, 16, left_t, 0)
-
-    def left_r(d, carry):
-        remote(part.at[0, 0], tsum_in.at[d], rsend.at[d], rrecv.at[d], partner).wait_send()
-        return carry
-
-    lax.fori_loop(1, 8, left_r, 0)
-
-    def left_g(d, carry):
-        remote(tall.at[0], tall.at[0], gsend.at[d], grecv.at[d], partner).wait_send()
-        return carry
-
-    lax.fori_loop(0, 15, left_g, 0)
 
     def left_w(j, carry):
         @pl.when(jnp.logical_not(jnp.logical_and(2 * j + c == s, s // 2 == h)))
@@ -726,11 +739,11 @@
             v((3, ROWS, HD), BF), v((3, ROWS, 2 * HD), BF), v((5, 3, ROWS, 2 * HD), BF),
             v((3, ROWS, HD), F32), v((3, ROWS, 2 * HD), F32), v((8, 3, ROWS, HD), BF),
             v((8, 2, 8, 3, 16, SHARD), BF), v((ROWS, PART), F32),
-            v((16, 16, 512), F32), v((16, 16, 512), F32), v((16, 16, PART), BF),
+            v((16, 16, 512), BF), v((16, 16, 512), BF), v((16, 16, PART), BF),
             v((16, 16, SHARD), F32), v((2, 8, 16, SHARD), F32),
             dma((11,)), dma((3, 19)), dma((3, 19)), dma((16,)), dma((16,)),
             dma((8,)), dma((8,)), dma((15,)), dma((15,)),
-            dma((5, 3)), dma((5, 3)), dma((9, 3)), dma((9, 3)),
+            dma((5, 3)), dma((5, 3)), dma((9, 4)), dma((9, 4)),
             dma((8,)), dma((8,)), dma((19,)), dma((19,)),
             dma((16,)), dma((16,)), dma((16,)), dma((16,)), dma((16,)), dma((2, 8)),
         ],

time: 126 us -> 122 us (0.968)
  Pallas kernels: 121 us -> 117 us
    pallas_call x1, Pallas kernels: 121 us -> 117 us  [block_kernel(): pl.pallas_call(kernel, name='attention_block', out_shape=(jax.ShapeDtypeS...]
where the time goes in v3:
time: 122 us; the launch traced here: 121 us
  Pallas kernels  117 us (96%)
  local copies, waits for them, and re-layouts  3.16 us (3%)
  between operations  1.29 us (1%)
    pallas_call x1, Pallas kernels, block_kernel(): pl.pallas_call(kernel, name='attention_block', out_shape=(jax.ShapeDtypeS...  117 us
    unnamed x2, local copies, waits for them, and re-layouts  3.16 us

profile of v3, /device:TPU:1, one launch (start us, length us, event | category | flops | bytes accessed | tf_op | source)
XLA Modules:
  0.0 121.5 jit_solution(11661767745314480976)
XLA Ops:
  1.3 117.0 %attention_block.1 = (bf16[640,384]{1,0:T(8,128)(2,1)}, bf16[16,384]{1,0:T(8,128)(2,1)}) custom-call(bf16[640,3072]{1,0:T(8,128)(2,1)} %vid_hbm.1, bf16[16,3072]{1,0:T(8,128)(2,1)} %txt.1, f32[3,3072]{1,0:T(4,128)} %modv.1, f32[3,3072]{1,0:T(4,128)} %modt.1, bf16[3,192,384]{2,1,0:T(8,128)(2,1)} %bitcast.5, bf16[3,192,384]{2,1,0:T(8,128)(2,1)} %bitcast.6, ...), custom_call_target="tpu_custom_call" | custom-call | tf_op jit(solution)/shard_map/attention_block/pallas_call | solution.py:726
  118.3 1.9 %copy.17 = bf16[640,384]{1,0:T(8,128)(2,1)} copy(bf16[640,384]{1,0:T(8,128)(2,1)} %get-tuple-element.4) | data formatting | bytes 983040
  120.2 1.3 %copy.18 = bf16[16,384]{1,0:T(8,128)(2,1)} copy(bf16[16,384]{1,0:T(8,128)(2,1)} %get-tuple-element.5) | data formatting | bytes 24576

commit v4 on v3

--- a/solution.py
+++ b/solution.py
@@ -581,13 +581,6 @@
     attend_other(2, 2)
     attend_other(3, 2)
     ring_two(0)
-    kv_arrive(4, 2)
-    attend_block(4, 2, (0, 3))
-    close_head(2)
-    attend_block(4, 2, (3, TILES))
-    close_head(3)
-    ring_one(1)
-    pg.two()
     def merge_wait(d, carry):
         remote(ts.at[0], ts_in.at[d], msend.at[d], mrecv.at[d], partner).wait_recv()
         return carry
@@ -621,36 +614,43 @@
 
     lax.fori_loop(1, 16, text_give, 0)
 
+    kv_arrive(4, 2)
+    attend_block(4, 2, (0, 3))
+    close_head(2)
+    attend_block(4, 2, (3, TILES))
+    close_head(3)
+    ring_one(1)
+    pg.two()
+    fetch_pt.wait()
+    def text_given(d, carry):
+        block = atg.at[(s + 16 - d) % 16]
+        remote(block, block, asend.at[d], arecv.at[d], partner).wait_recv()
+        return carry
+
+    lax.fori_loop(1, 16, text_given, 0)
+    tpart[...] = lax.dot_general(
+        atg[...].reshape(256, PART), pt[...], (((1,), (1,)), ((), ())),
+        preferred_element_type=F32).reshape(16, 16, SHARD)
+
+    def text_move(i, carry):
+        here = jnp.logical_and(i == s, s // 2 == h)
+
+        @pl.when(jnp.logical_not(here))
+        def _():
+            remote(tpart.at[i], tpart_in.at[c, h], osend.at[i], orecv.at[c, h], i, s // 2).start()
+
+        @pl.when(here)
+        def _():
+            pltpu.make_async_copy(tpart.at[i], tpart_in.at[c, h], own_sem.at[3]).start()
+        return carry
+
+    lax.fori_loop(0, 16, text_move, 0)
+
     ring_one(2)
     ring_two(1)
     ring_one(3)
     ring_two(2)
     pg.three()
-    fetch_pt.wait()
-    def text_given(d, carry):
-        block = atg.at[(s + 16 - d) % 16]
-        remote(block, block, asend.at[d], arecv.at[d], partner).wait_recv()
-        return carry
-
-    lax.fori_loop(1, 16, text_given, 0)
-    tpart[...] = lax.dot_general(
-        atg[...].reshape(256, PART), pt[...], (((1,), (1,)), ((), ())),
-        preferred_element_type=F32).reshape(16, 16, SHARD)
-
-    def text_move(i, carry):
-        here = jnp.logical_and(i == s, s // 2 == h)
-
-        @pl.when(jnp.logical_not(here))
-        def _():
-            remote(tpart.at[i], tpart_in.at[c, h], osend.at[i], orecv.at[c, h], i, s // 2).start()
-
-        @pl.when(here)
-        def _():
-            pltpu.make_async_copy(tpart.at[i], tpart_in.at[c, h], own_sem.at[3]).start()
-        return carry
-
-    lax.fori_loop(0, 16, text_move, 0)
-
     ring_two(3)
     for place in ("O", "Y", "L", "R", "LY", "RY", "D", "DY"):
         pg.pair(place)

time: 122 us -> 121 us (level)
  no operation moved by 1% of the time
where the time goes in v4:
time: 121 us
  Pallas kernels  116 us (96%)
  local copies, waits for them, and re-layouts  3.16 us (3%)
  between operations  1.29 us (1%)
    pallas_call x1, Pallas kernels, block_kernel(): pl.pallas_call(kernel, name='attention_block', out_shape=(jax.ShapeDtypeS...  116 us
    unnamed x2, local copies, waits for them, and re-layouts  3.16 us

profile of v4, /device:TPU:1, one launch (start us, length us, event | category | flops | bytes accessed | tf_op | source)
XLA Modules:
  0.0 120.6 jit_solution(18256723377467079044)
XLA Ops:
  1.3 116.2 %attention_block.1 = (bf16[640,384]{1,0:T(8,128)(2,1)}, bf16[16,384]{1,0:T(8,128)(2,1)}) custom-call(bf16[640,3072]{1,0:T(8,128)(2,1)} %vid_hbm.1, bf16[16,3072]{1,0:T(8,128)(2,1)} %txt.1, f32[3,3072]{1,0:T(4,128)} %modv.1, f32[3,3072]{1,0:T(4,128)} %modt.1, bf16[3,192,384]{2,1,0:T(8,128)(2,1)} %bitcast.5, bf16[3,192,384]{2,1,0:T(8,128)(2,1)} %bitcast.6, ...), custom_call_target="tpu_custom_call" | custom-call | tf_op jit(solution)/shard_map/attention_block/pallas_call | solution.py:726
  117.4 1.9 %copy.17 = bf16[640,384]{1,0:T(8,128)(2,1)} copy(bf16[640,384]{1,0:T(8,128)(2,1)} %get-tuple-element.4) | data formatting | bytes 983040
  119.3 1.3 %copy.18 = bf16[16,384]{1,0:T(8,128)(2,1)} copy(bf16[16,384]{1,0:T(8,128)(2,1)} %get-tuple-element.5) | data formatting | bytes 24576
